TPU v7x, 32 devices: a whole 2x2x4 slice. The times are simulated.
32 devices in a mesh: group: 2 (over y), lon: 4 (over z), lat: 2 (over x), fld: 2 (over core).
Axes of the slice: x: 2, y: 2, z: 4, core: 2. Of those that a mesh axis runs over, the one named last changes fastest.
Arguments:
- background: float32 [8, 32, 8192], P('group', ('lat', 'fld'), 'lon'), parts along dimension 0, may hold values from -7.2 to 7.2
- decay_sq: float32 [4, 32, 8192], P(None, ('lat', 'fld'), 'lon'), may hold values from 0.02 to 0.5
- edge_weight: float32 [4, 32, 8192], P(None, ('lat', 'fld'), 'lon'), may hold values from 0.1 to 1
- coupling: float32 [4, 4], replicated, may hold values from -0.32 to 1.6, as said below
- obs_tiles: bfloat16 [256, 256, 256], P(('lon', 'lat', 'fld')), may hold values from -0.375 to 0.375
- obs_values: float32 [512, 256], P(('group', 'lon', 'lat', 'fld')), parts along dimension 0, may hold values from -15 to 15
- obs_weights: float32 [256, 256], P(('lon', 'lat', 'fld')), may hold values from 4 to 32
- obs_counts: int32 [256], P(('lon', 'lat', 'fld')), may hold values from 32 to 256, as said below
- swath_ids: int32 [256], P(('lon', 'lat', 'fld')), may hold values from 0 to 7
- swath_scale: float32 [8], replicated, may hold values from 0.5 to 2
- tile_owner: int32 [256], P(('lon', 'lat', 'fld')), may hold values from 0 to 3, as said below
- tile_slot: int32 [256], P(('lon', 'lat', 'fld')), may hold values from 0 to 255
Outputs:
- solution: float32 [8, 32, 8192], P('group', ('lat', 'fld'), 'lon'), parts along dimension 0
- residual: float32 [8, 32, 8192], P('group', ('lat', 'fld'), 'lon'), parts along dimension 0
There are 2 independent parts, one for each index of `group`. A program takes and returns all parts, laid end to end along the dimension named above; an argument that names none is the same for every part. Nothing has to cross between parts.
Inputs may be any that keep to these rules, and one draw needn't show every extreme that they name: `obs_counts`: each device's 16 tiles include one with all 256 observations live. `tile_owner`: of one device's 16 tiles at most 4 read patches in any one longitude block, and in every block row some longitude block is read by exactly 4 tiles of each device of that block row. `coupling`: Symmetric, each diagonal entry above the sum of the magnitudes of its row's others.
All inputs are finite; a program needn't handle non-finite values.
Results may differ from a plain program's by a relative error of at most 0.0065.
Values may be sent and summed in bfloat16 or wider, within the bound.
A program may use at most 64 MiB of HBM per device.

v0:
```python
import jax
import jax.numpy as jnp
from jax import lax
from jax.sharding import PartitionSpec as P

CAP = 4
ITERS = 3


DIRECTIONS = ((0, 1), (1, 0), (1, 1), (1, -1))


def extended(shard, sides, width):
    for axis, dim in sides:
        count, length = (lax.axis_size(axis), shard.shape[dim])
        up = [(i, (i + 1) % count) for i in range(count)]
        down = [(j, i) for i, j in up]
        last = lax.slice_in_dim(shard, length - width, length, axis=dim)
        leading = lax.slice_in_dim(shard, 0, width, axis=dim)
        before = lax.ppermute(last, axis, up)
        after = lax.ppermute(leading, axis, down)
        shard = jnp.concatenate([before, shard, after], axis=dim)
    return shard


def stencil(padded, weights_pad, decay_part):
    rows_out = decay_part.shape[-2]
    cols_out = decay_part.shape[-1]

    def window_at(source, step_lat, step_lon):
        return source[
            ..., 1 + step_lat : 1 + step_lat + rows_out, 1 + step_lon : 1 + step_lon + cols_out
        ]

    center = window_at(padded, 0, 0)
    summed = decay_part * center
    for index_dir in range(4):
        step_lat, step_lon = DIRECTIONS[index_dir]
        weight_here = window_at(weights_pad[index_dir], 0, 0)
        weight_ahead = 0.5 * (weight_here + window_at(weights_pad[index_dir], step_lat, step_lon))
        weight_behind = 0.5 * (
            weight_here + window_at(weights_pad[index_dir], -step_lat, -step_lon)
        )
        summed = summed + weight_ahead * (center - window_at(padded, step_lat, step_lon))
        summed = summed + weight_behind * (center - window_at(padded, -step_lat, -step_lon))
    return summed


def mix_fields(coupling, field_in):
    return jnp.einsum("fg,gyx->fyx", coupling, field_in, precision=lax.Precision.HIGHEST)


def close_rows(padded, pad_depth, row_index, lat_rows, total_rows):
    global_row = row_index * lat_rows - pad_depth + jnp.arange(padded.shape[-2])
    inside = (global_row >= 0) & (global_row < total_rows)
    return jnp.where(inside[:, None], padded, 0.0)


def on_device(
    background,
    decay_sq,
    edge_weight,
    coupling,
    obs_tiles,
    obs_values,
    obs_weights,
    obs_counts,
    swath_ids,
    swath_scale,
    tile_owner,
    tile_slot,
):
    fields, lat_rows, lon_cells = background.shape
    tiles_here, obs_len, patch_len = obs_tiles.shape
    lon_count = lax.axis_size("lon")
    row_index = lax.axis_index(("lat", "fld"))
    total_rows = lax.axis_size(("lat", "fld")) * lat_rows
    patch_count = fields * lat_rows * lon_cells // patch_len
    stacked = jnp.concatenate([decay_sq, edge_weight], axis=0)
    coef_pad = extended(stacked, (("lon", 2), (("lat", "fld"), 1)), 2)
    coef_pad = close_rows(coef_pad, 2, row_index, lat_rows, total_rows)
    weights_two = coef_pad[fields:]
    weights_one = weights_two[:, 1:-1, 1:-1]

    def pad_state(field_in):
        padded = extended(field_in, (("lon", 2), (("lat", "fld"), 1)), 1)
        return close_rows(padded, 1, row_index, lat_rows, total_rows)

    def prior_apply(field_in):
        first_pass = stencil(pad_state(field_in), weights_one, decay_sq)
        return stencil(pad_state(mix_fields(coupling, first_pass)), weights_one, decay_sq)

    tile_order = jnp.arange(tiles_here)
    same_dest = (tile_owner[:, None] == tile_owner[None, :]) & (
        tile_order[None, :] < tile_order[:, None]
    )
    rank_within = jnp.sum(same_dest.astype(jnp.int32), axis=1)
    position = tile_owner * CAP + rank_within
    asked = jnp.zeros((lon_count * CAP,), jnp.int32).at[position].set(tile_slot)
    requested = lax.all_to_all(
        asked.reshape(lon_count, CAP), "lon", split_axis=0, concat_axis=0, tiled=True
    ).reshape(-1)
    lookup = jnp.sum(
        jnp.where(
            swath_ids[:, None] == jnp.arange(swath_scale.shape[0])[None, :],
            swath_scale[None, :],
            0.0,
        ),
        axis=1,
    )
    live_rows = jnp.arange(obs_len)[None, :] < obs_counts[:, None]
    weight_eff = jnp.where(live_rows, obs_weights * lookup[:, None], 0.0)

    def send_back(contribution):
        outgoing = (
            jnp.zeros((lon_count * CAP, patch_len), jnp.float32).at[position].set(contribution)
        )
        arrived = lax.all_to_all(
            outgoing.reshape(lon_count, CAP, patch_len),
            "lon",
            split_axis=0,
            concat_axis=0,
            tiled=True,
        )
        placed = (
            jnp.zeros((patch_count, patch_len), jnp.float32)
            .at[requested]
            .add(arrived.reshape(-1, patch_len))
        )
        return placed.reshape(fields, lat_rows, lon_cells)

    def squares(field_in):
        return lax.psum(jnp.sum(field_in * field_in), ("lon", "lat", "fld"))

    scaled_obs = (weight_eff * obs_values).astype(jnp.bfloat16)
    obs_side = jnp.einsum("top,to->tp", obs_tiles, scaled_obs, preferred_element_type=jnp.float32)
    right_side = prior_apply(background) + send_back(obs_side)
    solution = jnp.zeros_like(right_side)
    residual = right_side
    direction = right_side
    norm_now = squares(residual)
    for iteration in range(ITERS):
        patch_rows = direction.reshape(patch_count, patch_len)[requested].astype(jnp.bfloat16)
        obs_arrived = lax.all_to_all(
            patch_rows.reshape(lon_count, CAP, patch_len),
            "lon",
            split_axis=0,
            concat_axis=0,
            tiled=True,
        )
        inputs = obs_arrived.reshape(-1, patch_len)[position]
        applied = jnp.einsum("top,tp->to", obs_tiles, inputs, preferred_element_type=jnp.float32)
        weighted = (weight_eff * applied).astype(jnp.bfloat16)
        obs_contribution = jnp.einsum(
            "top,to->tp", obs_tiles, weighted, preferred_element_type=jnp.float32
        )
        applied = prior_apply(direction) + send_back(obs_contribution)
        curvature = lax.psum(jnp.sum(direction * applied), ("lon", "lat", "fld"))
        step_size = norm_now / curvature
        solution = solution + step_size * direction
        residual = residual - step_size * applied
        norm_next = squares(residual)
        direction = residual + norm_next / norm_now * direction
        norm_now = norm_next
    return (solution, residual)


def solution(mesh):
    return jax.shard_map(
        on_device,
        mesh=mesh,
        in_specs=(
            P("group", ("lat", "fld"), "lon"),
            P(None, ("lat", "fld"), "lon"),
            P(None, ("lat", "fld"), "lon"),
            P(),
            P(("lon", "lat", "fld"), None, None),
            P(("group", "lon", "lat", "fld"), None),
            P(("lon", "lat", "fld"), None),
            P(("lon", "lat", "fld")),
            P(("lon", "lat", "fld")),
            P(),
            P(("lon", "lat", "fld")),
            P(("lon", "lat", "fld")),
        ),
        out_specs=(P("group", ("lat", "fld"), "lon"), P("group", ("lat", "fld"), "lon")),
        check_vma=False,
    )
```

profile of v0, /device:TPU:0, one launch (start us, length us, event | category | flops | bytes accessed | tf_op | source)
XLA Modules:
  0.0 372.8 jit_solution(11629821197567600617)
XLA Ops:
  2.8 3.1 collective-permute-start.4
  5.9 2.1 collective-permute-start.5
  9.2 3.8 %collective-permute-start.1 = (f32[4,8,1]{2,0,1:T(4,128)S(1)}, f32[4,8,1]{2,0,1:T(4,128)S(1)}, u32[]{:S(2)}, u32[]{:S(2)}) collective-permute-start(f32[4,8,1]{2,0,1:T(4,128)S(1)} %get-tuple-element.61), channel_id=1, source_target_pairs={{4,0},{8,4},{12,8},{0,12},{5,1},{9,5},{13,9},{1,13},{6,2},{10,6},{... | collective-permute-start | bytes 392 | tf_op jit(solution)/shard_map/ppermute | solution.py:21
  16.0 3.2 all-to-all-start
  24.7 3.9 %all-to-all-start.1 = ((f32[4,4,256]{2,1,0:T(4,128)}), f32[4,4,256]{2,1,0:T(4,128)S(1)}, u32[]{:S(2)}, u32[]{:S(2)}) async-start(f32[4,4,256]{2,1,0:T(4,128)} %reshape.118), calls=%async_computation.1 | async-start | bytes 32768 | tf_op jit(solution)/shard_map/all_to_all | solution.py:118
  30.8 1.7 collective-permute-start.3
  34.1 1.8 collective-permute-start.7
  36.0 2.5 collective-permute-done.6
  40.3 1.4 convolution_bitcast_fusion.3
  41.8 2.0 collective-permute-start.8
  43.8 1.9 collective-permute-start.9
  48.8 1.7 collective-permute-start.11
  54.3 1.9 fusion.125
  57.7 2.6 collective-permute-start.13
  61.7 3.2 all-to-all-start.2
  65.9 1.7 collective-permute-start.15
  67.6 2.8 all-to-all-done.2
  72.0 1.4 convolution_bitcast_fusion.2
  74.2 3.2 collective-permute-start.17
  77.5 1.8 collective-permute-done.16
  81.2 1.7 collective-permute-start.19
  84.1 10.3 %all_to_all.44 = f32[4,4,256]{2,1,0:T(4,128)S(1)} all-to-all(f32[4,4,256]{2,1,0:T(4,128)S(1)} %reshape.123), channel_id=1, replica_groups=mesh['group'=2,'lon'=4,'lat'=2,'fld'=2] {'lon'}, dimensions={0} | all-to-all | bytes 32768 | tf_op jit(solution)/shard_map/all_to_all | solution.py:118
  94.4 1.5 scatter_custom_fusion.4
  95.9 1.7 reshape.125
  97.8 2.5 multiply_reduce_fusion.4
  100.2 30.1 %all-reduce = (f32[]{:T(128)}, f32[]{:T(128)}) all-reduce(f32[]{:T(128)} %get-tuple-element.13, f32[]{:T(128)} %get-tuple-element.12), channel_id=1, replica_groups=mesh['group'=2,'lon'=4,'lat'=2,'fld'=2] {'lon','lat','fld'}, use_global_device_ids=true, to_apply=%region_6.7 | all-reduce | flops 2 | bytes 16 | tf_op jit(solution)/shard_map/psum | solution.py:133
  132.4 30.2 %psum.44 = f32[]{:T(128)} all-reduce(f32[]{:T(128)} %multiply_reduce_fusion.3), channel_id=1, replica_groups=mesh['group'=2,'lon'=4,'lat'=2,'fld'=2] {'lon','lat','fld'}, use_global_device_ids=true, to_apply=%region_12.13 | all-reduce | flops 1 | bytes 8 | tf_op jit(solution)/shard_map/psum | solution.py:133
  165.5 3.8 %collective-permute-start.21 = (f32[4,8,1]{2,0,1:T(4,128)}, f32[4,8,1]{2,0,1:T(4,128)}, u32[]{:S(2)}, u32[]{:S(2)}) collective-permute-start(f32[4,8,1]{2,0,1:T(4,128)} %get-tuple-element.53), channel_id=1, source_target_pairs={{4,0},{8,4},{12,8},{0,12},{5,1},{9,5},{13,9},{1,13},{6,2},{10,6},{... | collective-permute-start | bytes 392 | tf_op jit(solution)/shard_map/ppermute | solution.py:21
  169.3 1.6 reshape.126
  170.9 1.6 gather_fusion.2
  173.2 3.2 all-to-all-start.4
  176.4 1.7 concatenate.68
  179.6 1.7 collective-permute-start.23
  184.6 1.4 convolution_bitcast_fusion.1
  186.9 1.6 collective-permute-start.24
  188.5 2.2 collective-permute-start.25
  190.8 1.7 collective-permute-done.24
  192.5 2.0 concatenate.70
  195.9 1.7 collective-permute-start.27
  200.1 10.7 %all_to_all.45 = f32[4,4,256]{2,1,0:T(4,128)S(1)} all-to-all(f32[4,4,256]{2,1,0:T(4,128)} %reshape.128), channel_id=1, replica_groups=mesh['group'=2,'lon'=4,'lat'=2,'fld'=2] {'lon'}, dimensions={0} | all-to-all | bytes 32768 | tf_op jit(solution)/shard_map/all_to_all | solution.py:118
  211.4 1.5 scatter_custom_fusion.6
  212.9 1.7 reshape.130
  215.8 3.2 multiply_reduce_fusion.2
  219.0 30.1 %psum.45 = f32[]{:T(128)} all-reduce(f32[]{:T(128)} %get-tuple-element.20), channel_id=1, replica_groups=mesh['group'=2,'lon'=4,'lat'=2,'fld'=2] {'lon','lat','fld'}, use_global_device_ids=true, to_apply=%region_16.17 | all-reduce | flops 1 | bytes 8 | tf_op jit(solution)/shard_map/psum | solution.py:158
  250.5 1.7 multiply_reduce_fusion.1
  252.2 30.1 %psum.46 = f32[]{:T(128)} all-reduce(f32[]{:T(128)} %get-tuple-element.18), channel_id=1, replica_groups=mesh['group'=2,'lon'=4,'lat'=2,'fld'=2] {'lon','lat','fld'}, use_global_device_ids=true, to_apply=%region_18.19 | all-reduce | flops 1 | bytes 8 | tf_op jit(solution)/shard_map/psum | solution.py:133
  285.1 3.8 %collective-permute-start.29 = (f32[4,8,1]{2,0,1:T(4,128)}, f32[4,8,1]{2,0,1:T(4,128)}, u32[]{:S(2)}, u32[]{:S(2)}) collective-permute-start(f32[4,8,1]{2,0,1:T(4,128)} %get-tuple-element.49), channel_id=1, source_target_pairs={{4,0},{8,4},{12,8},{0,12},{5,1},{9,5},{13,9},{1,13},{6,2},{10,6},{... | collective-permute-start | bytes 392 | tf_op jit(solution)/shard_map/ppermute | solution.py:21
  288.9 1.6 reshape.131
  290.5 1.6 gather_fusion.4
  292.8 3.2 all-to-all-start.6
  296.0 1.7 concatenate.72
  299.2 1.7 collective-permute-start.31
  304.3 1.4 convolution_bitcast_fusion
  306.5 1.6 collective-permute-start.32
  308.1 2.2 collective-permute-start.33
  310.4 1.7 collective-permute-done.32
  312.1 2.0 concatenate.74
  314.1 1.4 fusion.274
  315.5 1.7 collective-permute-start.35
  319.7 10.7 %all_to_all.46 = f32[4,4,256]{2,1,0:T(4,128)S(1)} all-to-all(f32[4,4,256]{2,1,0:T(4,128)} %reshape.133), channel_id=1, replica_groups=mesh['group'=2,'lon'=4,'lat'=2,'fld'=2] {'lon'}, dimensions={0} | all-to-all | bytes 32768 | tf_op jit(solution)/shard_map/all_to_all | solution.py:118
  331.0 1.5 scatter_custom_fusion.8
  332.5 1.7 reshape.135
  335.4 3.3 multiply_reduce_fusion
  338.7 30.1 %psum.47 = f32[]{:T(128)} all-reduce(f32[]{:T(128)} %get-tuple-element.16), channel_id=1, replica_groups=mesh['group'=2,'lon'=4,'lat'=2,'fld'=2] {'lon','lat','fld'}, use_global_device_ids=true, to_apply=%region_22.23 | all-reduce | flops 1 | bytes 8 | tf_op jit(solution)/shard_map/psum | solution.py:158
  (238 shorter events, 62.0 us)
Async XLA Ops:
  0.6 21.3 %copy-start = (bf16[16,256,256]{2,1,0:T(8,128)(2,1)S(1)}, bf16[16,256,256]{2,1,0:T(8,128)(2,1)}, u32[]{:S(2)}) copy-start(bf16[16,256,256]{2,1,0:T(8,128)(2,1)} %param.16) | copy-start | bytes 6291460
  2.7 27.7 %copy-start.18 = (f32[8,8,2048]{2,1,0:T(8,128)}, f32[8,8,2048]{2,1,0:T(8,128)S(1)}, u32[]{:S(2)}) copy-start(f32[8,8,2048]{2,1,0:T(8,128)S(1)} %constant_dynamic-update-slice_fusion) | copy-start | bytes 1572868
  2.8 29.7 %collective-permute-start.4 = (f32[8,8,2]{2,1,0:T(8,128)S(1)}, f32[8,8,2]{2,1,0:T(8,128)S(1)}, u32[]{:S(2)}, u32[]{:S(2)}) collective-permute-start(f32[8,8,2]{2,1,0:T(8,128)S(1)} %get-tuple-element.30), channel_id=1, source_target_pairs={{0,4},{4,8},{8,12},{12,0},{1,5},{5,9},{9,13},{13,1},{2,6},{6,10},{... | collective-permute-start | bytes 1544 | tf_op jit(solution)/shard_map/ppermute | solution.py:20
  5.9 26.7 %collective-permute-start.5 = (f32[8,8,2]{2,1,0:T(8,128)S(1)}, f32[8,8,2]{2,1,0:T(8,128)S(1)}, u32[]{:S(2)}, u32[]{:S(2)}) collective-permute-start(f32[8,8,2]{2,1,0:T(8,128)S(1)} %get-tuple-element.29), channel_id=1, source_target_pairs={{4,0},{8,4},{12,8},{0,12},{5,1},{9,5},{13,9},{1,13},{6,2},{10,6},{... | collective-permute-start | bytes 1544 | tf_op jit(solution)/shard_map/ppermute | solution.py:21
  9.2 21.2 %collective-permute-start = (f32[4,8,1]{2,0,1:T(4,128)S(1)}, f32[4,8,1]{2,0,1:T(4,128)S(1)}, u32[]{:S(2)}, u32[]{:S(2)}) collective-permute-start(f32[4,8,1]{2,0,1:T(4,128)S(1)} %get-tuple-element.62), channel_id=1, source_target_pairs={{0,4},{4,8},{8,12},{12,0},{1,5},{5,9},{9,13},{13,1},{2,6},{6,10},{... | collective-permute-start | bytes 392 | tf_op jit(solution)/shard_map/ppermute | solution.py:20
  9.2 21.2 %collective-permute-start.1 = (f32[4,8,1]{2,0,1:T(4,128)S(1)}, f32[4,8,1]{2,0,1:T(4,128)S(1)}, u32[]{:S(2)}, u32[]{:S(2)}) collective-permute-start(f32[4,8,1]{2,0,1:T(4,128)S(1)} %get-tuple-element.61), channel_id=1, source_target_pairs={{4,0},{8,4},{12,8},{0,12},{5,1},{9,5},{13,9},{1,13},{6,2},{10,6},{... | collective-permute-start | bytes 392 | tf_op jit(solution)/shard_map/ppermute | solution.py:21
  14.6 14.0 %copy-start.38 = (s32[16]{0:T(128)}, s32[16]{0:T(128)S(1)}, u32[]{:S(2)}) copy-start(s32[16]{0:T(128)S(1)} %compare_select_fusion.1) | copy-start | bytes 196
  16.0 8.7 %all-to-all-start = ((s32[4,1,4]{2,1,0:T(1,128)}), s32[4,1,4]{2,1,0:T(1,128)S(1)}, u32[]{:S(2)}, u32[]{:S(2)}) async-start(s32[4,1,4]{2,1,0:T(1,128)} %bitcast.6), calls=%async_computation | async-start | bytes 4096 | tf_op jit(solution)/shard_map/all_to_all | solution.py:100
  20.3 15.6 %copy-start.25 = (pred[10]{0:T(512)(128)(4,1)}, pred[10]{0:T(512)(128)(4,1)S(1)}, u32[]{:S(2)}) copy-start(pred[10]{0:T(512)(128)(4,1)S(1)} %compare_and_fusion.1) | copy-start | bytes 34
  21.1 12.9 %copy-start.33 = (f32[16]{0:T(128)}, f32[16]{0:T(128)S(1)}, u32[]{:S(2)}) copy-start(f32[16]{0:T(128)S(1)} %select_reduce_fusion) | copy-start | bytes 196
  24.7 27.2 %all-to-all-start.1 = ((f32[4,4,256]{2,1,0:T(4,128)}), f32[4,4,256]{2,1,0:T(4,128)S(1)}, u32[]{:S(2)}, u32[]{:S(2)}) async-start(f32[4,4,256]{2,1,0:T(4,128)} %reshape.118), calls=%async_computation.1 | async-start | bytes 32768 | tf_op jit(solution)/shard_map/all_to_all | solution.py:118
  30.4 8.9 %copy-start.37 = (pred[12]{0:T(512)(128)(4,1)S(1)}, pred[12]{0:T(512)(128)(4,1)}, u32[]{:S(2)}) copy-start(pred[12]{0:T(512)(128)(4,1)} %compare_and_fusion) | copy-start | bytes 40
  30.7 5.2 %collective-permute-start.2 = (f32[4,1,2050]{2,0,1:T(4,128)S(1)}, f32[4,1,2050]{2,0,1:T(4,128)S(1)}, u32[]{:S(2)}, u32[]{:S(2)}) collective-permute-start(f32[4,1,2050]{2,0,1:T(4,128)S(1)} %get-tuple-element.45), channel_id=1, source_target_pairs={{0,1},{1,2},{2,3},{3,0},{4,5},{5,6},{6,7},{7,4},{8,9},{9,10},{10,1... | collective-permute-start | bytes 98408 | tf_op jit(solution)/shard_map/ppermute | solution.py:20
  30.8 5.1 %collective-permute-start.3 = (f32[4,1,2050]{2,0,1:T(4,128)S(1)}, f32[4,1,2050]{2,0,1:T(4,128)S(1)}, u32[]{:S(2)}, u32[]{:S(2)}) collective-permute-start(f32[4,1,2050]{2,0,1:T(4,128)S(1)} %get-tuple-element.46), channel_id=1, source_target_pairs={{1,0},{2,1},{3,2},{0,3},{5,4},{6,5},{7,6},{4,7},{9,8},{10,9},{11,1... | collective-permute-start | bytes 98408 | tf_op jit(solution)/shard_map/ppermute | solution.py:21
  34.0 4.5 %collective-permute-start.6 = (f32[8,2,2052]{2,0,1:T(8,128)S(1)}, f32[8,2,2052]{2,0,1:T(8,128)S(1)}, u32[]{:S(2)}, u32[]{:S(2)}) collective-permute-start(f32[8,2,2052]{2,0,1:T(8,128)S(1)} %copy.102), channel_id=1, source_target_pairs={{0,1},{1,2},{2,3},{3,0},{4,5},{5,6},{6,7},{7,4},{8,9},{9,10},{10,1... | collective-permute-start | bytes 393992 | tf_op jit(solution)/shard_map/ppermute | solution.py:20
  34.1 5.1 %collective-permute-start.7 = (f32[8,2,2052]{2,0,1:T(8,128)S(1)}, f32[8,2,2052]{2,0,1:T(8,128)S(1)}, u32[]{:S(2)}, u32[]{:S(2)}) collective-permute-start(f32[8,2,2052]{2,0,1:T(8,128)S(1)} %copy.103), channel_id=1, source_target_pairs={{1,0},{2,1},{3,2},{0,3},{5,4},{6,5},{7,6},{4,7},{9,8},{10,9},{11,1... | collective-permute-start | bytes 393992 | tf_op jit(solution)/shard_map/ppermute | solution.py:21
  40.0 175.7 %copy-start.2 = (f32[8,2048]{1,0:T(8,128)}, f32[8,2048]{1,0:T(8,128)S(1)}, u32[]{:S(2)}) copy-start(f32[8,2048]{1,0:T(8,128)S(1)} %get-tuple-element.73) | copy-start | bytes 196612
  40.0 175.7 %copy-start.4 = (f32[8,2048]{1,0:T(8,128)}, f32[8,2048]{1,0:T(8,128)S(1)}, u32[]{:S(2)}) copy-start(f32[8,2048]{1,0:T(8,128)S(1)} %get-tuple-element.74) | copy-start | bytes 196612
  40.1 57.6 %copy-start.10 = (f32[8,2048]{1,0:T(8,128)}, f32[8,2048]{1,0:T(8,128)S(1)}, u32[]{:S(2)}) copy-start(f32[8,2048]{1,0:T(8,128)S(1)} %get-tuple-element.71) | copy-start | bytes 196612
  40.2 57.6 %copy-start.13 = (f32[8,2048]{1,0:T(8,128)}, f32[8,2048]{1,0:T(8,128)S(1)}, u32[]{:S(2)}) copy-start(f32[8,2048]{1,0:T(8,128)S(1)} %get-tuple-element.72) | copy-start | bytes 196612
  40.2 175.6 %copy-start.6 = (f32[8,2048]{1,0:T(8,128)}, f32[8,2048]{1,0:T(8,128)S(1)}, u32[]{:S(2)}) copy-start(f32[8,2048]{1,0:T(8,128)S(1)} %get-tuple-element.69) | copy-start | bytes 196612
  40.2 175.6 %copy-start.8 = (f32[8,2048]{1,0:T(8,128)}, f32[8,2048]{1,0:T(8,128)S(1)}, u32[]{:S(2)}) copy-start(f32[8,2048]{1,0:T(8,128)S(1)} %get-tuple-element.70) | copy-start | bytes 196612
  40.3 5.4 %copy-start.39 = (s32[16,1]{0,1:T(1,128)S(1)}, s32[16,1]{0,1:T(1,128)}, u32[]{:S(2)}) copy-start(s32[16,1]{0,1:T(1,128)} %reshape.117) | copy-start | bytes 196
  40.3 13.9 %copy-start.26 = (pred[10]{0:T(512)(128)(4,1)S(1)}, pred[10]{0:T(512)(128)(4,1)}, u32[]{:S(2)}) copy-start(pred[10]{0:T(512)(128)(4,1)} %copy-done.25) | copy-start | bytes 34
  41.8 5.5 %collective-permute-start.8 = (f32[4,8,1]{2,0,1:T(4,128)S(1)}, f32[4,8,1]{2,0,1:T(4,128)S(1)}, u32[]{:S(2)}, u32[]{:S(2)}) collective-permute-start(f32[4,8,1]{2,0,1:T(4,128)S(1)} %get-tuple-element.60), channel_id=1, source_target_pairs={{0,4},{4,8},{8,12},{12,0},{1,5},{5,9},{9,13},{13,1},{2,6},{6,10},{... | collective-permute-start | bytes 392 | tf_op jit(solution)/shard_map/ppermute | solution.py:20
  43.8 4.0 %collective-permute-start.9 = (f32[4,8,1]{2,0,1:T(4,128)S(1)}, f32[4,8,1]{2,0,1:T(4,128)S(1)}, u32[]{:S(2)}, u32[]{:S(2)}) collective-permute-start(f32[4,8,1]{2,0,1:T(4,128)S(1)} %get-tuple-element.59), channel_id=1, source_target_pairs={{4,0},{8,4},{12,8},{0,12},{5,1},{9,5},{13,9},{1,13},{6,2},{10,6},{... | collective-permute-start | bytes 392 | tf_op jit(solution)/shard_map/ppermute | solution.py:21
  48.8 5.3 %collective-permute-start.10 = (f32[4,1,2050]{2,0,1:T(4,128)}, f32[4,1,2050]{2,0,1:T(4,128)S(1)}, u32[]{:S(2)}, u32[]{:S(2)}) collective-permute-start(f32[4,1,2050]{2,0,1:T(4,128)} %get-tuple-element.43), channel_id=1, source_target_pairs={{0,1},{1,2},{2,3},{3,0},{4,5},{5,6},{6,7},{7,4},{8,9},{9,10},{10,1... | collective-permute-start | bytes 98408 | tf_op jit(solution)/shard_map/ppermute | solution.py:20
  48.8 5.3 %collective-permute-start.11 = (f32[4,1,2050]{2,0,1:T(4,128)S(1)}, f32[4,1,2050]{2,0,1:T(4,128)S(1)}, u32[]{:S(2)}, u32[]{:S(2)}) collective-permute-start(f32[4,1,2050]{2,0,1:T(4,128)S(1)} %get-tuple-element.44), channel_id=1, source_target_pairs={{1,0},{2,1},{3,2},{0,3},{5,4},{6,5},{7,6},{4,7},{9,8},{10,9},{11,1... | collective-permute-start | bytes 98408 | tf_op jit(solution)/shard_map/ppermute | solution.py:21
  56.4 15.6 %copy-start.41 = (f32[4,4]{1,0:T(4,128)S(1)}, f32[4,4]{1,0:T(4,128)}, u32[]{:S(2)}) copy-start(f32[4,4]{1,0:T(4,128)} %param.15) | copy-start | bytes 196
  56.4 8.5 %collective-permute-start.12 = (f32[4,8,1]{2,0,1:T(4,128)S(1)}, f32[4,8,1]{2,0,1:T(4,128)S(1)}, u32[]{:S(2)}, u32[]{:S(2)}) collective-permute-start(f32[4,8,1]{2,0,1:T(4,128)S(1)} %get-tuple-element.58), channel_id=1, source_target_pairs={{0,4},{4,8},{8,12},{12,0},{1,5},{5,9},{9,13},{13,1},{2,6},{6,10},{... | collective-permute-start | bytes 392 | tf_op jit(solution)/shard_map/ppermute | solution.py:20
  57.7 7.2 %collective-permute-start.13 = (f32[4,8,1]{2,0,1:T(4,128)S(1)}, f32[4,8,1]{2,0,1:T(4,128)S(1)}, u32[]{:S(2)}, u32[]{:S(2)}) collective-permute-start(f32[4,8,1]{2,0,1:T(4,128)S(1)} %get-tuple-element.57), channel_id=1, source_target_pairs={{4,0},{8,4},{12,8},{0,12},{5,1},{9,5},{13,9},{1,13},{6,2},{10,6},{... | collective-permute-start | bytes 392 | tf_op jit(solution)/shard_map/ppermute | solution.py:21
  61.7 8.8 %all-to-all-start.2 = ((bf16[4,4,256]{2,1,0:T(4,128)(2,1)}), bf16[4,4,256]{2,1,0:T(4,128)(2,1)S(1)}, u32[]{:S(2)}, u32[]{:S(2)}) async-start(bf16[4,4,256]{2,1,0:T(4,128)(2,1)} %convert_element_type.39), calls=%async_computation.2 | async-start | bytes 16384 | tf_op jit(solution)/shard_map/all_to_all | solution.py:144
  65.9 5.9 %collective-permute-start.14 = (f32[4,1,2050]{2,0,1:T(4,128)}, f32[4,1,2050]{2,0,1:T(4,128)S(1)}, u32[]{:S(2)}, u32[]{:S(2)}) collective-permute-start(f32[4,1,2050]{2,0,1:T(4,128)} %get-tuple-element.41), channel_id=1, source_target_pairs={{0,1},{1,2},{2,3},{3,0},{4,5},{5,6},{6,7},{7,4},{8,9},{9,10},{10,1... | collective-permute-start | bytes 98408 | tf_op jit(solution)/shard_map/ppermute | solution.py:20
  65.9 5.9 %collective-permute-start.15 = (f32[4,1,2050]{2,0,1:T(4,128)}, f32[4,1,2050]{2,0,1:T(4,128)S(1)}, u32[]{:S(2)}, u32[]{:S(2)}) collective-permute-start(f32[4,1,2050]{2,0,1:T(4,128)} %get-tuple-element.42), channel_id=1, source_target_pairs={{1,0},{2,1},{3,2},{0,3},{5,4},{6,5},{7,6},{4,7},{9,8},{10,9},{11,1... | collective-permute-start | bytes 98408 | tf_op jit(solution)/shard_map/ppermute | solution.py:21
  73.5 5.8 %copy-start.20 = (f32[4,8,2048]{2,0,1:T(4,128)}, f32[4,8,2048]{2,0,1:T(4,128)S(1)}, u32[]{:S(2)}) copy-start(f32[4,8,2048]{2,0,1:T(4,128)S(1)} %convolution_bitcast_fusion.2) | copy-start | bytes 786436
  73.5 24.1 %copy-start.27 = (pred[10]{0:T(512)(128)(4,1)S(1)}, pred[10]{0:T(512)(128)(4,1)}, u32[]{:S(2)}) copy-start(pred[10]{0:T(512)(128)(4,1)} %copy-done.25) | copy-start | bytes 34
  73.6 5.7 %collective-permute-start.16 = (f32[4,8,1]{2,0,1:T(4,128)S(1)}, f32[4,8,1]{2,0,1:T(4,128)S(1)}, u32[]{:S(2)}, u32[]{:S(2)}) collective-permute-start(f32[4,8,1]{2,0,1:T(4,128)S(1)} %get-tuple-element.56), channel_id=1, source_target_pairs={{0,4},{4,8},{8,12},{12,0},{1,5},{5,9},{9,13},{13,1},{2,6},{6,10},{... | collective-permute-start | bytes 392 | tf_op jit(solution)/shard_map/ppermute | solution.py:20
  74.2 5.1 %collective-permute-start.17 = (f32[4,8,1]{2,0,1:T(4,128)S(1)}, f32[4,8,1]{2,0,1:T(4,128)S(1)}, u32[]{:S(2)}, u32[]{:S(2)}) collective-permute-start(f32[4,8,1]{2,0,1:T(4,128)S(1)} %get-tuple-element.55), channel_id=1, source_target_pairs={{4,0},{8,4},{12,8},{0,12},{5,1},{9,5},{13,9},{1,13},{6,2},{10,6},{... | collective-permute-start | bytes 392 | tf_op jit(solution)/shard_map/ppermute | solution.py:21
  81.2 16.4 %collective-permute-start.18 = (f32[4,1,2050]{2,0,1:T(4,128)}, f32[4,1,2050]{2,0,1:T(4,128)S(1)}, u32[]{:S(2)}, u32[]{:S(2)}) collective-permute-start(f32[4,1,2050]{2,0,1:T(4,128)} %get-tuple-element.39), channel_id=1, source_target_pairs={{0,1},{1,2},{2,3},{3,0},{4,5},{5,6},{6,7},{7,4},{8,9},{9,10},{10,1... | collective-permute-start | bytes 98408 | tf_op jit(solution)/shard_map/ppermute | solution.py:20
  81.2 16.4 %collective-permute-start.19 = (f32[4,1,2050]{2,0,1:T(4,128)}, f32[4,1,2050]{2,0,1:T(4,128)S(1)}, u32[]{:S(2)}, u32[]{:S(2)}) collective-permute-start(f32[4,1,2050]{2,0,1:T(4,128)} %get-tuple-element.40), channel_id=1, source_target_pairs={{1,0},{2,1},{3,2},{0,3},{5,4},{6,5},{7,6},{4,7},{9,8},{10,9},{11,1... | collective-permute-start | bytes 98408 | tf_op jit(solution)/shard_map/ppermute | solution.py:21
  165.5 10.9 %collective-permute-start.20 = (f32[4,8,1]{2,0,1:T(4,128)}, f32[4,8,1]{2,0,1:T(4,128)}, u32[]{:S(2)}, u32[]{:S(2)}) collective-permute-start(f32[4,8,1]{2,0,1:T(4,128)} %get-tuple-element.54), channel_id=1, source_target_pairs={{0,4},{4,8},{8,12},{12,0},{1,5},{5,9},{9,13},{13,1},{2,6},{6,10},{... | collective-permute-start | bytes 392 | tf_op jit(solution)/shard_map/ppermute | solution.py:20
  165.5 10.9 %collective-permute-start.21 = (f32[4,8,1]{2,0,1:T(4,128)}, f32[4,8,1]{2,0,1:T(4,128)}, u32[]{:S(2)}, u32[]{:S(2)}) collective-permute-start(f32[4,8,1]{2,0,1:T(4,128)} %get-tuple-element.53), channel_id=1, source_target_pairs={{4,0},{8,4},{12,8},{0,12},{5,1},{9,5},{13,9},{1,13},{6,2},{10,6},{... | collective-permute-start | bytes 392 | tf_op jit(solution)/shard_map/ppermute | solution.py:21
  173.2 8.8 %all-to-all-start.4 = ((bf16[4,4,256]{2,1,0:T(4,128)(2,1)}), bf16[4,4,256]{2,1,0:T(4,128)(2,1)S(1)}, u32[]{:S(2)}, u32[]{:S(2)}) async-start(bf16[4,4,256]{2,1,0:T(4,128)(2,1)} %convert_element_type.42), calls=%async_computation.4 | async-start | bytes 16384 | tf_op jit(solution)/shard_map/all_to_all | solution.py:144
  179.6 3.8 %collective-permute-start.22 = (f32[4,1,2050]{2,0,1:T(4,128)}, f32[4,1,2050]{2,0,1:T(4,128)}, u32[]{:S(2)}, u32[]{:S(2)}) collective-permute-start(f32[4,1,2050]{2,0,1:T(4,128)} %get-tuple-element.37), channel_id=1, source_target_pairs={{0,1},{1,2},{2,3},{3,0},{4,5},{5,6},{6,7},{7,4},{8,9},{9,10},{10,1... | collective-permute-start | bytes 98408 | tf_op jit(solution)/shard_map/ppermute | solution.py:20
  179.6 3.8 %collective-permute-start.23 = (f32[4,1,2050]{2,0,1:T(4,128)}, f32[4,1,2050]{2,0,1:T(4,128)}, u32[]{:S(2)}, u32[]{:S(2)}) collective-permute-start(f32[4,1,2050]{2,0,1:T(4,128)} %get-tuple-element.38), channel_id=1, source_target_pairs={{1,0},{2,1},{3,2},{0,3},{5,4},{6,5},{7,6},{4,7},{9,8},{10,9},{11,1... | collective-permute-start | bytes 98408 | tf_op jit(solution)/shard_map/ppermute | solution.py:21
  184.6 6.1 %copy-start.23 = (f32[16,256]{1,0:T(8,128)S(1)}, f32[16,256]{1,0:T(8,128)}, u32[]{:S(2)}) copy-start(f32[16,256]{1,0:T(8,128)} %param.18) | copy-start | bytes 49156
  184.6 6.1 %copy-start.31 = (s32[16]{0:T(128)S(1)}, s32[16]{0:T(128)}, u32[]{:S(2)}) copy-start(s32[16]{0:T(128)} %param.19) | copy-start | bytes 196
  184.6 6.1 %copy-start.35 = (f32[16]{0:T(128)S(1)}, f32[16]{0:T(128)}, u32[]{:S(2)}) copy-start(f32[16]{0:T(128)} %copy-done.33) | copy-start | bytes 196
  186.9 5.6 %collective-permute-start.24 = (f32[4,8,1]{2,0,1:T(4,128)S(1)}, f32[4,8,1]{2,0,1:T(4,128)}, u32[]{:S(2)}, u32[]{:S(2)}) collective-permute-start(f32[4,8,1]{2,0,1:T(4,128)S(1)} %get-tuple-element.52), channel_id=1, source_target_pairs={{0,4},{4,8},{8,12},{12,0},{1,5},{5,9},{9,13},{13,1},{2,6},{6,10},{... | collective-permute-start | bytes 392 | tf_op jit(solution)/shard_map/ppermute | solution.py:20
  188.5 4.0 %collective-permute-start.25 = (f32[4,8,1]{2,0,1:T(4,128)S(1)}, f32[4,8,1]{2,0,1:T(4,128)}, u32[]{:S(2)}, u32[]{:S(2)}) collective-permute-start(f32[4,8,1]{2,0,1:T(4,128)S(1)} %get-tuple-element.51), channel_id=1, source_target_pairs={{4,0},{8,4},{12,8},{0,12},{5,1},{9,5},{13,9},{1,13},{6,2},{10,6},{... | collective-permute-start | bytes 392 | tf_op jit(solution)/shard_map/ppermute | solution.py:21
  195.9 18.7 %collective-permute-start.26 = (f32[4,1,2050]{2,0,1:T(4,128)}, f32[4,1,2050]{2,0,1:T(4,128)}, u32[]{:S(2)}, u32[]{:S(2)}) collective-permute-start(f32[4,1,2050]{2,0,1:T(4,128)} %get-tuple-element.35), channel_id=1, source_target_pairs={{0,1},{1,2},{2,3},{3,0},{4,5},{5,6},{6,7},{7,4},{8,9},{9,10},{10,1... | collective-permute-start | bytes 98408 | tf_op jit(solution)/shard_map/ppermute | solution.py:20
  195.9 18.7 %collective-permute-start.27 = (f32[4,1,2050]{2,0,1:T(4,128)}, f32[4,1,2050]{2,0,1:T(4,128)}, u32[]{:S(2)}, u32[]{:S(2)}) collective-permute-start(f32[4,1,2050]{2,0,1:T(4,128)} %get-tuple-element.36), channel_id=1, source_target_pairs={{1,0},{2,1},{3,2},{0,3},{5,4},{6,5},{7,6},{4,7},{9,8},{10,9},{11,1... | collective-permute-start | bytes 98408 | tf_op jit(solution)/shard_map/ppermute | solution.py:21
  285.1 10.9 %collective-permute-start.28 = (f32[4,8,1]{2,0,1:T(4,128)}, f32[4,8,1]{2,0,1:T(4,128)}, u32[]{:S(2)}, u32[]{:S(2)}) collective-permute-start(f32[4,8,1]{2,0,1:T(4,128)} %get-tuple-element.50), channel_id=1, source_target_pairs={{0,4},{4,8},{8,12},{12,0},{1,5},{5,9},{9,13},{13,1},{2,6},{6,10},{... | collective-permute-start | bytes 392 | tf_op jit(solution)/shard_map/ppermute | solution.py:20
  285.1 10.9 %collective-permute-start.29 = (f32[4,8,1]{2,0,1:T(4,128)}, f32[4,8,1]{2,0,1:T(4,128)}, u32[]{:S(2)}, u32[]{:S(2)}) collective-permute-start(f32[4,8,1]{2,0,1:T(4,128)} %get-tuple-element.49), channel_id=1, source_target_pairs={{4,0},{8,4},{12,8},{0,12},{5,1},{9,5},{13,9},{1,13},{6,2},{10,6},{... | collective-permute-start | bytes 392 | tf_op jit(solution)/shard_map/ppermute | solution.py:21
  292.8 8.8 %all-to-all-start.6 = ((bf16[4,4,256]{2,1,0:T(4,128)(2,1)}), bf16[4,4,256]{2,1,0:T(4,128)(2,1)S(1)}, u32[]{:S(2)}, u32[]{:S(2)}) async-start(bf16[4,4,256]{2,1,0:T(4,128)(2,1)} %convert_element_type.45), calls=%async_computation.6 | async-start | bytes 16384 | tf_op jit(solution)/shard_map/all_to_all | solution.py:144
  299.2 3.8 %collective-permute-start.30 = (f32[4,1,2050]{2,0,1:T(4,128)}, f32[4,1,2050]{2,0,1:T(4,128)}, u32[]{:S(2)}, u32[]{:S(2)}) collective-permute-start(f32[4,1,2050]{2,0,1:T(4,128)} %get-tuple-element.33), channel_id=1, source_target_pairs={{0,1},{1,2},{2,3},{3,0},{4,5},{5,6},{6,7},{7,4},{8,9},{9,10},{10,1... | collective-permute-start | bytes 98408 | tf_op jit(solution)/shard_map/ppermute | solution.py:20
  299.2 3.8 %collective-permute-start.31 = (f32[4,1,2050]{2,0,1:T(4,128)}, f32[4,1,2050]{2,0,1:T(4,128)}, u32[]{:S(2)}, u32[]{:S(2)}) collective-permute-start(f32[4,1,2050]{2,0,1:T(4,128)} %get-tuple-element.34), channel_id=1, source_target_pairs={{1,0},{2,1},{3,2},{0,3},{5,4},{6,5},{7,6},{4,7},{9,8},{10,9},{11,1... | collective-permute-start | bytes 98408 | tf_op jit(solution)/shard_map/ppermute | solution.py:21
  304.2 6.1 %copy-start.24 = (f32[16,256]{1,0:T(8,128)S(1)}, f32[16,256]{1,0:T(8,128)}, u32[]{:S(2)}) copy-start(f32[16,256]{1,0:T(8,128)} %param.18) | copy-start | bytes 49156
  304.2 6.1 %copy-start.32 = (s32[16]{0:T(128)S(1)}, s32[16]{0:T(128)}, u32[]{:S(2)}) copy-start(s32[16]{0:T(128)} %param.19) | copy-start | bytes 196
  304.3 6.1 %copy-start.36 = (f32[16]{0:T(128)S(1)}, f32[16]{0:T(128)}, u32[]{:S(2)}) copy-start(f32[16]{0:T(128)} %copy-done.33) | copy-start | bytes 196
  306.5 5.6 %collective-permute-start.32 = (f32[4,8,1]{2,0,1:T(4,128)S(1)}, f32[4,8,1]{2,0,1:T(4,128)}, u32[]{:S(2)}, u32[]{:S(2)}) collective-permute-start(f32[4,8,1]{2,0,1:T(4,128)S(1)} %get-tuple-element.48), channel_id=1, source_target_pairs={{0,4},{4,8},{8,12},{12,0},{1,5},{5,9},{9,13},{13,1},{2,6},{6,10},{... | collective-permute-start | bytes 392 | tf_op jit(solution)/shard_map/ppermute | solution.py:20
  308.1 4.0 %collective-permute-start.33 = (f32[4,8,1]{2,0,1:T(4,128)S(1)}, f32[4,8,1]{2,0,1:T(4,128)}, u32[]{:S(2)}, u32[]{:S(2)}) collective-permute-start(f32[4,8,1]{2,0,1:T(4,128)S(1)} %get-tuple-element.47), channel_id=1, source_target_pairs={{4,0},{8,4},{12,8},{0,12},{5,1},{9,5},{13,9},{1,13},{6,2},{10,6},{... | collective-permute-start | bytes 392 | tf_op jit(solution)/shard_map/ppermute | solution.py:21
  315.5 18.7 %collective-permute-start.34 = (f32[4,1,2050]{2,0,1:T(4,128)}, f32[4,1,2050]{2,0,1:T(4,128)}, u32[]{:S(2)}, u32[]{:S(2)}) collective-permute-start(f32[4,1,2050]{2,0,1:T(4,128)} %get-tuple-element.31), channel_id=1, source_target_pairs={{0,1},{1,2},{2,3},{3,0},{4,5},{5,6},{6,7},{7,4},{8,9},{9,10},{10,1... | collective-permute-start | bytes 98408 | tf_op jit(solution)/shard_map/ppermute | solution.py:20
  315.5 18.7 %collective-permute-start.35 = (f32[4,1,2050]{2,0,1:T(4,128)}, f32[4,1,2050]{2,0,1:T(4,128)}, u32[]{:S(2)}, u32[]{:S(2)}) collective-permute-start(f32[4,1,2050]{2,0,1:T(4,128)} %get-tuple-element.32), channel_id=1, source_target_pairs={{1,0},{2,1},{3,2},{0,3},{5,4},{6,5},{7,6},{4,7},{9,8},{10,9},{11,1... | collective-permute-start | bytes 98408 | tf_op jit(solution)/shard_map/ppermute | solution.py:21
  (21 other events, 41.8 us)
where the time goes:
time: 375 us; the launch traced here: 373 us
  blocking collectives  182 us (49%)
  starting transfers between devices  68.6 us (18%)
  local copies, waits for them, and re-layouts  56.1 us (15%)
  other arithmetic  31.9 us (9%)
  waiting for transfers between devices  15.3 us (4%)
  matrix products  10.4 us (3%)
  between operations  8.24 us (2%)
    psum x3, blocking collectives, squares(): return lax.psum(jnp.sum(field_in * field_in), ('lon', 'lat', 'fld'))  90.4 us
    psum x2, blocking collectives, on_device(): curvature = lax.psum(jnp.sum(direction * applied), ('lon', 'lat', 'fld'))  60.2 us
    ppermute x18, starting transfers between devices, extended(): after = lax.ppermute(leading, axis, down)  41.3 us
    all_to_all x3, blocking collectives, send_back(): lax.all_to_all(outgoing.reshape(lon_count, CAP, patch_len), 'lon', split_...  31.7 us
    concatenate x9, local copies, waits for them, and re-layouts, extended(): shard = jnp.concatenate([before, shard, after], axis=dim)  11 us
    ppermute x18, starting transfers between devices, extended(): before = lax.ppermute(last, axis, up)  10.4 us
    all_to_all x3, starting transfers between devices, on_device(): lax.all_to_all(patch_rows.reshape(lon_count, CAP, patch_len), 'lon', spli...  9.71 us
    reduce_sum x3, other arithmetic, on_device(): curvature = lax.psum(jnp.sum(direction * applied), ('lon', 'lat', 'fld'))  9.02 us
  transfers between devices with their start and end apart: 41, of which 11 were waited for; matrix products, arithmetic and copies ran while one was open for 15% of the time, Pallas kernels for 0%

commit v1 on v0

v1 whole, which is shorter than its diff:
```python
import functools

import jax
import jax.numpy as jnp
from jax import lax
from jax.experimental import pallas as pl
from jax.experimental.pallas import tpu as pltpu
from jax.sharding import PartitionSpec as P

CAP = 4
ITERS = 3
SLOT_ROWS = 8
EDGE = 128
MESH = pl.DeviceIdType.MESH


def loop(low, high, body):
    if high - low <= 4:
        for k in range(low, high):
            body(k)
    else:
        lax.fori_loop(low, high, lambda k, c: (body(k), c)[1], 0)


def kernel(
    sizes,
    owner_s,
    slot_s,
    counts_s,
    swath_s,
    scale_s,
    coupling_s,
    bg,
    decay,
    edge,
    tiles_hbm,
    obs_values,
    obs_weights,
    sol_out,
    res_out,
    tiles,
    ve,
    hn,
    hs,
    p0,
    p7,
    coef,
    diag,
    pe,
    pn,
    ps_,
    weight,
    ask,
    req,
    gather_oh,
    scatter_oh,
    xs,
    xr,
    xp,
    zs,
    zr,
    qp,
    part,
    parts,
    halo_send,
    halo_recv,
    ex_send,
    ex_recv,
    red_send,
    red_recv,
    load_sem,
):
    lon_n, lat_n, fld_n = sizes
    row_n = lat_n * fld_n
    dev_n = lon_n * row_n
    fields, rows, cols = bg.shape
    tile_n, obs_len, patch = tiles.shape
    ext = cols + 2 * EDGE
    per_row = cols // patch
    patch_n = fields * rows * per_row
    pos_n = lon_n * SLOT_ROWS
    bf16, f32 = jnp.bfloat16, jnp.float32

    my_lon = lax.axis_index("lon")
    my_row = lax.axis_index("lat") * fld_n + lax.axis_index("fld")
    me = my_lon * row_n + my_row

    def device(lon, row):
        return {"lon": lon, "lat": row // fld_n, "fld": row % fld_n}

    west, east = (my_lon + lon_n - 1) % lon_n, (my_lon + 1) % lon_n
    north, south = (my_row + row_n - 1) % row_n, (my_row + 1) % row_n
    has_north = (my_row > 0).astype(f32)
    has_south = (my_row < row_n - 1).astype(f32)

    load = pltpu.make_async_copy(tiles_hbm, tiles, load_sem)
    load.start()

    barrier = pltpu.get_barrier_semaphore()

    def greet(k):
        other = (me + k) % dev_n
        pl.semaphore_signal(
            barrier, inc=1, device_id=device(other // row_n, other % row_n), device_id_type=MESH
        )

    loop(1, dev_n, greet)

    center = pl.ds(EDGE, cols)
    left, right = pl.ds(0, EDGE), pl.ds(EDGE + cols, EDGE)
    first, final = pl.ds(0, EDGE), pl.ds(cols - EDGE, EDGE)

    def halo_copies(h):
        pairs = (
            (ve.at[h, :, :, pl.ds(EDGE, EDGE)], ve.at[h, :, :, right], west, my_row),
            (ve.at[h, :, :, pl.ds(cols, EDGE)], ve.at[h, :, :, left], east, my_row),
            (p0.at[h], hs.at[h, :, center], my_lon, north),
            (p7.at[h], hn.at[h, :, center], my_lon, south),
            (p0.at[h, :, first], hs.at[h, :, right], west, north),
            (p0.at[h, :, final], hs.at[h, :, left], east, north),
            (p7.at[h, :, first], hn.at[h, :, right], west, south),
            (p7.at[h, :, final], hn.at[h, :, left], east, south),
        )
        return [
            pltpu.make_async_remote_copy(
                src_ref=src,
                dst_ref=dst,
                send_sem=halo_send.at[h, k],
                recv_sem=halo_recv.at[h, k],
                device_id=device(lon, row),
                device_id_type=MESH,
            )
            for k, (src, dst, lon, row) in enumerate(pairs)
        ]

    def put_field(h, f, value):
        ve[h, f, :, EDGE : EDGE + cols] = value
        p0[h, f : f + 1, :] = value[0:1]
        p7[h, f : f + 1, :] = value[rows - 1 : rows]

    def halo_start(h):
        for copy in halo_copies(h):
            copy.start()

    def halo_wait(h):
        for copy in halo_copies(h):
            copy.wait_recv()

    def swap_start(number, out, into):
        def send(k):
            to = (my_lon + k) % lon_n
            pltpu.make_async_remote_copy(
                src_ref=out.at[to],
                dst_ref=into.at[my_lon],
                send_sem=ex_send.at[number],
                recv_sem=ex_recv.at[number],
                device_id=device(to, my_row),
                device_id_type=MESH,
            ).start()

        loop(1, lon_n, send)
        into[my_lon] = out[my_lon]

    def swap_wait(sems, number, buffer):
        some = buffer.at[pl.ds(0, lon_n - 1)]
        pltpu.make_async_copy(some, some, sems.at[number]).wait()

    def total_start(number, value):
        part[number] = value
        parts[number, me] = value

        def send(k):
            other = (me + k) % dev_n
            pltpu.make_async_remote_copy(
                src_ref=part.at[number],
                dst_ref=parts.at[number, me],
                send_sem=red_send.at[number],
                recv_sem=red_recv.at[number],
                device_id=device(other // row_n, other % row_n),
                device_id_type=MESH,
            ).start()

        loop(1, dev_n, send)

    def total_wait(sems, number):
        some = parts.at[number, pl.ds(0, dev_n - 1)]
        pltpu.make_async_copy(some, some, sems.at[number]).wait()

    def total(number):
        total_wait(red_recv, number)
        lanes = jnp.sum(parts[number], axis=0)
        return jnp.sum(lanes, axis=1, keepdims=True)

    def lanes_of(value):
        lane_sum = value[:, 0:128]
        for k in range(1, value.shape[1] // 128):
            lane_sum = lane_sum + value[:, k * 128 : (k + 1) * 128]
        return jnp.sum(lane_sum, axis=0, keepdims=True)

    sub = lax.broadcasted_iota(jnp.int32, (rows, ext), 0)

    def above(value, halo):
        return jnp.where(sub == 0, halo, pltpu.roll(value, 1, 0))

    def below(value, halo):
        return jnp.where(sub == rows - 1, halo, pltpu.roll(value, rows - 1, 0))

    def apply_l(f, value, up_halo, down_halo):
        up, down = above(value, up_halo), below(value, down_halo)
        toward_east = coef[0] * value + coef[1] * up + coef[2] * down
        toward_west = coef[3] * value + coef[4] * up + coef[5] * down
        result = diag[f] * value - coef[6] * up - coef[7] * down
        result = result - pltpu.roll(toward_east, ext - 1, 1) - pltpu.roll(toward_west, 1, 1)
        return result[:, EDGE : EDGE + cols]

    def mixed(first_pass, f):
        acc = coupling_s[f, 0] * first_pass[0]
        for g in range(1, fields):
            acc = acc + coupling_s[f, g] * first_pass[g]
        return acc

    def split3(value):
        high = value.astype(bf16)
        rest = value - high.astype(f32)
        middle = rest.astype(bf16)
        return high, middle, (rest - middle.astype(f32)).astype(bf16)

    row_iota = lax.broadcasted_iota(jnp.int32, (pos_n, 128), 0)
    wide_iota = lax.broadcasted_iota(jnp.int32, (pos_n, patch), 0)
    obs_iota = lax.broadcasted_iota(jnp.int32, (pos_n, obs_len), 1)

    for f in range(fields):
        put_field(0, f, bg[f])
    for e in range(4):
        put_field(1, e, edge[e])

    positions = []
    for t in range(tile_n):
        rank = jnp.int32(0)
        for other in range(t):
            rank = rank + (owner_s[other] == owner_s[t]).astype(jnp.int32)
        positions.append(owner_s[t] * SLOT_ROWS + rank)

    asked = jnp.full((pos_n, 128), -1, jnp.int32)
    weight_all = jnp.zeros((pos_n, obs_len), f32)
    values_all = jnp.zeros((pos_n, obs_len), f32)
    for t in range(tile_n):
        number = slot_s[t]
        column, rest = number % per_row, number // per_row
        moved = (column * fields + rest // rows) * rows + rest % rows
        asked = jnp.where(row_iota == positions[t], moved, asked)
        here = wide_iota == positions[t]
        live = here & (obs_iota < counts_s[t])
        weight_all = jnp.where(
            live, obs_weights[t : t + 1, :] * scale_s[swath_s[t]], weight_all
        )
        values_all = jnp.where(here, obs_values[t : t + 1, :], values_all)
    ask[...] = asked.reshape(lon_n, SLOT_ROWS, 128)
    weight[...] = weight_all

    def spread(value, t):
        return jnp.where(wide_iota == positions[t], value, 0.0).astype(bf16)

    def forward(value):
        acc = None
        for t in range(tile_n):
            term = lax.dot_general(
                spread(value, t), tiles[t], (((1,), (1,)), ((), ())), preferred_element_type=f32
            )
            acc = term if acc is None else acc + term
        return acc

    def adjoint(value):
        acc = None
        for t in range(tile_n):
            term = lax.dot_general(
                spread(value, t), tiles[t], (((1,), (0,)), ((), ())), preferred_element_type=f32
            )
            acc = term if acc is None else acc + term
        return acc

    pl.semaphore_wait(barrier, dev_n - 1)
    halo_start(1)
    halo_start(0)
    swap_start(0, ask, req)

    load.wait()
    scaled = (weight_all * values_all).astype(bf16).astype(f32)
    zs[0] = adjoint(scaled).reshape(lon_n, SLOT_ROWS, patch)
    swap_start(1, zs.at[0], zr.at[0])

    halo_wait(1)
    w = [ve[1, e] for e in range(4)]
    w_up = [above(w[e], hn[1, e : e + 1, :] * has_north) for e in range(4)]
    w_down = [below(w[e], hs[1, e : e + 1, :] * has_south) for e in range(4)]
    w_west = {e: pltpu.roll(w[e], 1, 1) for e in (0, 2, 3)}
    w_east = {e: pltpu.roll(w[e], ext - 1, 1) for e in (0, 2, 3)}
    e0, e1, e2 = (
        0.5 * (w_west[0] + w[0]),
        0.5 * (w_west[3] + w_up[3]),
        0.5 * (w_west[2] + w_down[2]),
    )
    v0, v1, v2 = (
        0.5 * (w_east[0] + w[0]),
        0.5 * (w_east[2] + w_up[2]),
        0.5 * (w_east[3] + w_down[3]),
    )
    n0, n1 = 0.5 * (w[1] + w_up[1]), 0.5 * (w[1] + w_down[1])
    for k, value in enumerate((e0, e1, e2, v0, v1, v2, n0, n1)):
        coef[k] = value
    degree = n0 + n1 + pltpu.roll(e0 + e1 + e2, ext - 1, 1) + pltpu.roll(v0 + v1 + v2, 1, 1)
    for f in range(fields):
        diag[f] = degree
        diag[f, :, EDGE : EDGE + cols] = decay[f] + degree[:, EDGE : EDGE + cols]

    def up_of(h, f):
        return hn[h, f : f + 1, :] * has_north

    def down_of(h, f):
        return hs[h, f : f + 1, :] * has_south

    halo_wait(0)
    first_pass = [apply_l(f, ve[0, f], up_of(0, f), down_of(0, f)) for f in range(fields)]
    for f in range(fields):
        put_field(2, f, mixed(first_pass, f))
    halo_start(2)

    swap_wait(ex_recv, 0, req)
    wanted = req[...].reshape(pos_n, 128)
    wanted = jnp.concatenate([wanted] * (patch_n // 128), axis=1)
    picked = wanted == lax.broadcasted_iota(jnp.int32, (pos_n, patch_n), 1)
    chosen = jnp.where(picked, 1.0, 0.0)
    gather_oh[...] = chosen.astype(bf16)
    if pos_n < 128:
        chosen = jnp.concatenate([chosen, jnp.zeros((128 - pos_n, patch_n), f32)], axis=0)
    scatter_oh[...] = chosen.T.astype(bf16)

    def placed(number):
        arrived = zr[number].reshape(pos_n, patch)
        if pos_n < 128:
            arrived = jnp.concatenate([arrived, jnp.zeros((128 - pos_n, patch), f32)], axis=0)
        high, middle, low = split3(arrived)
        return (
            jnp.dot(scatter_oh[...], low, preferred_element_type=f32)
            + jnp.dot(scatter_oh[...], middle, preferred_element_type=f32)
        ) + jnp.dot(scatter_oh[...], high, preferred_element_type=f32)

    def placed_field(blocks, f):
        return jnp.concatenate(
            [
                blocks[(c * fields + f) * rows : (c * fields + f + 1) * rows]
                for c in range(per_row)
            ],
            axis=1,
        )

    halo_wait(2)
    second = [apply_l(f, ve[2, f], up_of(2, f), down_of(2, f)) for f in range(fields)]
    for f in range(fields):
        qp[f] = second[f]
    swap_wait(ex_recv, 1, zr.at[0])
    blocks = placed(0)
    for f in range(fields):
        put_field(3, f, qp[f] + placed_field(blocks, f))
        sol_out[f] = jnp.zeros((rows, cols), f32)
    pe[...] = jnp.zeros_like(pe)
    pn[...] = jnp.zeros_like(pn)
    ps_[...] = jnp.zeros_like(ps_)
    xp[...] = jnp.zeros_like(xp)

    def iterate(it, norm_before):
        h_r, h_u = 3 + 2 * it, 4 + 2 * it
        halo_start(h_r)
        squares = jnp.zeros((1, 128), f32)
        for f in range(fields):
            value = ve[h_r, f, :, EDGE : EDGE + cols]
            squares = squares + lanes_of(value * value)
        total_start(2 * it, squares)
        stacked = jnp.concatenate(
            [
                ve[h_r, f, :, EDGE + c * patch : EDGE + (c + 1) * patch]
                for c in range(per_row)
                for f in range(fields)
            ],
            axis=0,
        )
        high, middle, low = split3(stacked)
        patches = (
            jnp.dot(gather_oh[...], low, preferred_element_type=f32)
            + jnp.dot(gather_oh[...], middle, preferred_element_type=f32)
        ) + jnp.dot(gather_oh[...], high, preferred_element_type=f32)
        xs[it] = patches.reshape(lon_n, SLOT_ROWS, patch)
        swap_start(2 + 2 * it, xs.at[it], xr.at[it])

        halo_wait(h_r)
        swap_wait(ex_recv, 2 + 2 * it, xr.at[it])
        norm = total(2 * it)
        ratio = norm / norm_before
        for f in range(fields):
            pe[f] = ve[h_r, f] + ratio * pe[f]
        pn[...] = hn[h_r] * has_north + ratio * pn[...]
        ps_[...] = hs[h_r] * has_south + ratio * ps_[...]
        seen = xr[it].reshape(pos_n, patch) + ratio * xp[...]
        xp[...] = seen

        first_pass = [
            apply_l(f, pe[f], pn[f : f + 1, :], ps_[f : f + 1, :]) for f in range(fields)
        ]
        curve = jnp.zeros((1, 128), f32)
        for f in range(fields):
            value = mixed(first_pass, f)
            put_field(h_u, f, value)
            curve = curve + lanes_of(value * first_pass[f])
        halo_start(h_u)

        applied = forward(seen)
        weighted = (weight[...] * applied).astype(bf16).astype(f32)
        curve = curve + lanes_of(applied * weighted)
        total_start(2 * it + 1, curve)
        zs[it + 1] = adjoint(weighted).reshape(lon_n, SLOT_ROWS, patch)
        swap_start(3 + 2 * it, zs.at[it + 1], zr.at[it + 1])

        halo_wait(h_u)
        for f in range(fields):
            qp[f] = apply_l(f, ve[h_u, f], up_of(h_u, f), down_of(h_u, f))
        swap_wait(ex_recv, 3 + 2 * it, zr.at[it + 1])
        blocks = placed(it + 1)
        step = norm / total(2 * it + 1)
        for f in range(fields):
            sol_out[f] = sol_out[f] + step * pe[f, :, EDGE : EDGE + cols]
            image = qp[f] + placed_field(blocks, f)
            put_field(h_r + 2, f, ve[h_r, f, :, EDGE : EDGE + cols] - step * image)
        return norm

    lax.fori_loop(0, ITERS, iterate, jnp.full((1, 1), 1.0, f32))
    for f in range(fields):
        res_out[f] = ve[3 + 2 * ITERS, f, :, EDGE : EDGE + cols]

    def sent_halo(h, carry):
        for copy in halo_copies(h):
            copy.wait_send()
        return carry

    lax.fori_loop(0, 3 + 2 * ITERS, sent_halo, 0)
    swap_wait(ex_send, 0, req)
    swap_wait(ex_send, 1, zr.at[0])

    def sent_rest(it, carry):
        swap_wait(ex_send, 2 + 2 * it, xr.at[it])
        swap_wait(ex_send, 3 + 2 * it, zr.at[it + 1])
        total_wait(red_send, 2 * it)
        total_wait(red_send, 2 * it + 1)
        return carry

    lax.fori_loop(0, ITERS, sent_rest, 0)


def on_device(
    sizes,
    background,
    decay_sq,
    edge_weight,
    coupling,
    obs_tiles,
    obs_values,
    obs_weights,
    obs_counts,
    swath_ids,
    swath_scale,
    tile_owner,
    tile_slot,
):
    fields, rows, cols = background.shape
    tile_n, obs_len, patch = obs_tiles.shape
    lon_n, lat_n, fld_n = sizes
    dev_n = lon_n * lat_n * fld_n
    ext = cols + 2 * EDGE
    pos_n = lon_n * SLOT_ROWS
    patch_n = fields * rows * cols // patch
    halos = 4 + 2 * ITERS
    f32, bf16 = jnp.float32, jnp.bfloat16
    smem = pl.BlockSpec(memory_space=pltpu.SMEM)
    vmem = pl.BlockSpec(memory_space=pltpu.VMEM)
    dma = pltpu.SemaphoreType.DMA
    shape = jax.ShapeDtypeStruct((fields, rows, cols), f32)
    return pl.pallas_call(
        functools.partial(kernel, sizes),
        out_shape=(shape, shape),
        in_specs=[smem] * 6 + [vmem] * 3 + [pl.BlockSpec(memory_space=pl.ANY)] + [vmem] * 2,
        out_specs=(vmem, vmem),
        scratch_shapes=[
            pltpu.VMEM((tile_n, obs_len, patch), bf16),
            pltpu.VMEM((halos, fields, rows, ext), f32),
            pltpu.VMEM((halos, fields, ext), f32),
            pltpu.VMEM((halos, fields, ext), f32),
            pltpu.VMEM((halos, fields, cols), f32),
            pltpu.VMEM((halos, fields, cols), f32),
            pltpu.VMEM((8, rows, ext), f32),
            pltpu.VMEM((fields, rows, ext), f32),
            pltpu.VMEM((fields, rows, ext), f32),
            pltpu.VMEM((fields, ext), f32),
            pltpu.VMEM((fields, ext), f32),
            pltpu.VMEM((pos_n, obs_len), f32),
            pltpu.VMEM((lon_n, SLOT_ROWS, 128), jnp.int32),
            pltpu.VMEM((lon_n, SLOT_ROWS, 128), jnp.int32),
            pltpu.VMEM((pos_n, patch_n), bf16),
            pltpu.VMEM((patch_n, 128), bf16),
            pltpu.VMEM((ITERS, lon_n, SLOT_ROWS, patch), f32),
            pltpu.VMEM((ITERS, lon_n, SLOT_ROWS, patch), f32),
            pltpu.VMEM((pos_n, patch), f32),
            pltpu.VMEM((ITERS + 1, lon_n, SLOT_ROWS, patch), f32),
            pltpu.VMEM((ITERS + 1, lon_n, SLOT_ROWS, patch), f32),
            pltpu.VMEM((fields, rows, cols), f32),
            pltpu.VMEM((2 * ITERS, 1, 128), f32),
            pltpu.VMEM((2 * ITERS, dev_n, 1, 128), f32),
            dma((halos, 8)),
            dma((halos, 8)),
            dma((2 + 2 * ITERS,)),
            dma((2 + 2 * ITERS,)),
            dma((2 * ITERS,)),
            dma((2 * ITERS,)),
            dma(()),
        ],
        compiler_params=pltpu.CompilerParams(
            collective_id=0, has_side_effects=True, vmem_limit_bytes=40 * 1024 * 1024
        ),
    )(
        tile_owner,
        tile_slot,
        obs_counts,
        swath_ids,
        swath_scale,
        coupling,
        background,
        decay_sq,
        edge_weight,
        obs_tiles,
        obs_values,
        obs_weights,
    )


def solution(mesh):
    sizes = (mesh.shape["lon"], mesh.shape["lat"], mesh.shape["fld"])
    return jax.shard_map(
        functools.partial(on_device, sizes),
        mesh=mesh,
        in_specs=(
            P("group", ("lat", "fld"), "lon"),
            P(None, ("lat", "fld"), "lon"),
            P(None, ("lat", "fld"), "lon"),
            P(),
            P(("lon", "lat", "fld"), None, None),
            P(("group", "lon", "lat", "fld"), None),
            P(("lon", "lat", "fld"), None),
            P(("lon", "lat", "fld")),
            P(("lon", "lat", "fld")),
            P(),
            P(("lon", "lat", "fld")),
            P(("lon", "lat", "fld")),
        ),
        out_specs=(P("group", ("lat", "fld"), "lon"), P("group", ("lat", "fld"), "lon")),
        check_vma=False,
    )
```

time: 375 us -> 65.1 us (0.17)
  blocking collectives: 182 us -> 0 us
  starting transfers between devices: 68.6 us -> 0 us
  Pallas kernels: 0 us -> 52.7 us
  local copies, waits for them, and re-layouts: 56.1 us -> 11.2 us
  other arithmetic: 31.9 us -> 0 us
  waiting for transfers between devices: 15.3 us -> 0 us
  matrix products: 10.4 us -> 0 us
  between operations: 8.24 us -> 0.66 us
    psum x5 -> x0, blocking collectives: 151 us -> none  [the longest x3 90.4 us: squares(): return lax.psum(jnp.sum(field_in * field_in), ('lon', 'lat', 'fld'))]
    pallas_call x0 -> x1, Pallas kernels: none -> 52.7 us  [on_device(): pl.pallas_call(functools.partial(kernel, sizes), out_shape=(shape, shape)...]
    ppermute x36 -> x0, starting transfers between devices: 51.7 us -> none  [the longest x18 41.3 us: extended(): after = lax.ppermute(leading, axis, down)]
    all_to_all x3 -> x0, blocking collectives: 31.7 us -> none  [send_back(): lax.all_to_all(outgoing.reshape(lon_count, CAP, patch_len), 'lon', split_...]
    all_to_all x5 -> x0, starting transfers between devices: 16.9 us -> none  [the longest x3 9.71 us: on_device(): lax.all_to_all(patch_rows.reshape(lon_count, CAP, patch_len), 'lon', spli...]
    reshape x19 -> x0, local copies, waits for them, and re-layouts: 13.5 us -> none  [the longest x4 5.84 us: send_back(): return placed.reshape(fields, lat_rows, lon_cells)]
    reduce_sum x7 -> x0, other arithmetic: 13.1 us -> none  [the longest x3 9.02 us: on_device(): curvature = lax.psum(jnp.sum(direction * applied), ('lon', 'lat', 'fld'))]
    concatenate x10 -> x0, local copies, waits for them, and re-layouts: 12 us -> none  [the longest x9 11 us: extended(): shard = jnp.concatenate([before, shard, after], axis=dim)]
  transfers between devices with their start and end apart: 41 -> 0, of which waited for: 11 -> 0; matrix products, arithmetic and copies ran while one was open for 15% -> 0% of each run, Pallas kernels for 0% -> 0%
where the time goes in v1:
time: 65.1 us; the launch traced here: 64.6 us
  Pallas kernels  52.7 us (81%)
  local copies, waits for them, and re-layouts  11.2 us (17%)
  between operations  0.66 us (1%)
    pallas_call x1, Pallas kernels, on_device(): pl.pallas_call(functools.partial(kernel, sizes), out_shape=(shape, shape)...  52.7 us
    unnamed x26, local copies, waits for them, and re-layouts  11.2 us

profile of v1, /device:TPU:0, one launch (start us, length us, event | category | flops | bytes accessed | tf_op | source)
XLA Modules:
  0.0 64.6 jit_solution(10708095808328524133)
XLA Ops:
  0.6 0.0 copy-start
  0.6 1.6 %copy-done = bf16[16,256,256]{2,1,0:T(8,128)(2,1)S(1)} copy-done((bf16[16,256,256]{2,1,0:T(8,128)(2,1)S(1)}, bf16[16,256,256]{2,1,0:T(8,128)(2,1)}, u32[]{:S(2)}) %copy-start) | copy-done | bytes 2097176
  2.2 0.0 copy-start.1
  2.2 0.9 %copy-done.1 = f32[4,8,2048]{2,1,0:T(8,128)S(1)} copy-done((f32[4,8,2048]{2,1,0:T(8,128)S(1)}, f32[4,8,2048]{2,1,0:T(8,128)}, u32[]{:S(2)}) %copy-start.1) | copy-done | bytes 262168
  3.2 0.0 copy-start.2
  3.2 0.9 %copy-done.2 = f32[4,8,2048]{2,1,0:T(8,128)S(1)} copy-done((f32[4,8,2048]{2,1,0:T(8,128)S(1)}, f32[4,8,2048]{2,1,0:T(8,128)}, u32[]{:S(2)}) %copy-start.2) | copy-done | bytes 262168
  4.1 0.0 copy-start.3
  4.1 0.9 %copy-done.3 = f32[4,8,2048]{2,1,0:T(8,128)S(1)} copy-done((f32[4,8,2048]{2,1,0:T(8,128)S(1)}, f32[4,8,2048]{2,1,0:T(8,128)}, u32[]{:S(2)}) %copy-start.3) | copy-done | bytes 262168
  5.1 0.0 copy-start.4
  5.1 0.7 %copy-done.4 = f32[16,256]{1,0:T(8,128)S(1)} copy-done((f32[16,256]{1,0:T(8,128)S(1)}, f32[16,256]{1,0:T(8,128)}, u32[]{:S(2)}) %copy-start.4) | copy-done | bytes 16408
  5.8 0.0 copy-start.5
  5.8 0.7 %copy-done.5 = f32[16,256]{1,0:T(8,128)S(1)} copy-done((f32[16,256]{1,0:T(8,128)S(1)}, f32[16,256]{1,0:T(8,128)}, u32[]{:S(2)}) %copy-start.5) | copy-done | bytes 16408
  6.5 0.0 copy-start.6
  6.5 0.7 %copy-done.6 = f32[4,4]{1,0:T(4,128)S(1)} copy-done((f32[4,4]{1,0:T(4,128)S(1)}, f32[4,4]{1,0:T(4,128)}, u32[]{:S(2)}) %copy-start.6) | copy-done | bytes 88
  7.2 0.0 copy-start.7
  7.2 0.7 %copy-done.7 = s32[16]{0:T(128)S(1)} copy-done((s32[16]{0:T(128)S(1)}, s32[16]{0:T(128)}, u32[]{:S(2)}) %copy-start.7) | copy-done | bytes 88
  7.9 0.0 copy-start.8
  7.9 0.7 %copy-done.8 = s32[16]{0:T(128)S(1)} copy-done((s32[16]{0:T(128)S(1)}, s32[16]{0:T(128)}, u32[]{:S(2)}) %copy-start.8) | copy-done | bytes 88
  8.5 0.0 copy-start.9
  8.5 0.7 %copy-done.9 = s32[16]{0:T(128)S(1)} copy-done((s32[16]{0:T(128)S(1)}, s32[16]{0:T(128)}, u32[]{:S(2)}) %copy-start.9) | copy-done | bytes 88
  9.2 0.0 copy-start.10
  9.2 0.7 %copy-done.10 = s32[16]{0:T(128)S(1)} copy-done((s32[16]{0:T(128)S(1)}, s32[16]{0:T(128)}, u32[]{:S(2)}) %copy-start.10) | copy-done | bytes 88
  9.8 0.0 copy-start.11
  9.8 0.7 %copy-done.11 = f32[8]{0:T(128)S(1)} copy-done((f32[8]{0:T(128)S(1)}, f32[8]{0:T(128)}, u32[]{:S(2)}) %copy-start.11) | copy-done | bytes 56
  10.5 52.7 %shard_map.131 = (f32[4,8,2048]{2,1,0:T(8,128)S(1)}, f32[4,8,2048]{2,1,0:T(8,128)S(1)}) custom-call(s32[16]{0:T(128)S(1)} %copy-done.7, s32[16]{0:T(128)S(1)} %copy-done.8, s32[16]{0:T(128)S(1)} %copy-done.9, s32[16]{0:T(128)S(1)} %copy-done.10, f32[8]{0:T(128)S(1)} %copy-done.11, f32[4,4]{1,0:T(4,128)S(1)} %copy-done.6, f32[4,8,2048]{2,1,0:T(8,128)S(1)} %copy-done.1, ...), custom_call_target="tpu_custom_call" | custom-call | tf_op jit(solution)/shard_map/pallas_call | solution.py:486
  63.2 0.7 %copy.16 = f32[4,8,2048]{2,1,0:T(8,128)} copy(f32[4,8,2048]{2,1,0:T(8,128)S(1)} %get-tuple-element.4) | data formatting | bytes 524288
  63.9 0.7 %copy.17 = f32[4,8,2048]{2,1,0:T(8,128)} copy(f32[4,8,2048]{2,1,0:T(8,128)S(1)} %get-tuple-element.5) | data formatting | bytes 524288
Async XLA Ops:
  0.6 1.6 %copy-start = (bf16[16,256,256]{2,1,0:T(8,128)(2,1)S(1)}, bf16[16,256,256]{2,1,0:T(8,128)(2,1)}, u32[]{:S(2)}) copy-start(bf16[16,256,256]{2,1,0:T(8,128)(2,1)} %tiles_hbm.1) | copy-start | bytes 6291460
  2.2 0.9 %copy-start.1 = (f32[4,8,2048]{2,1,0:T(8,128)S(1)}, f32[4,8,2048]{2,1,0:T(8,128)}, u32[]{:S(2)}) copy-start(f32[4,8,2048]{2,1,0:T(8,128)} %bg.1) | copy-start | bytes 786436
  3.2 0.9 %copy-start.2 = (f32[4,8,2048]{2,1,0:T(8,128)S(1)}, f32[4,8,2048]{2,1,0:T(8,128)}, u32[]{:S(2)}) copy-start(f32[4,8,2048]{2,1,0:T(8,128)} %decay.1) | copy-start | bytes 786436
  4.1 0.9 %copy-start.3 = (f32[4,8,2048]{2,1,0:T(8,128)S(1)}, f32[4,8,2048]{2,1,0:T(8,128)}, u32[]{:S(2)}) copy-start(f32[4,8,2048]{2,1,0:T(8,128)} %edge.1) | copy-start | bytes 786436
  5.1 0.7 %copy-start.4 = (f32[16,256]{1,0:T(8,128)S(1)}, f32[16,256]{1,0:T(8,128)}, u32[]{:S(2)}) copy-start(f32[16,256]{1,0:T(8,128)} %obs_values.1) | copy-start | bytes 49156
  5.8 0.7 %copy-start.5 = (f32[16,256]{1,0:T(8,128)S(1)}, f32[16,256]{1,0:T(8,128)}, u32[]{:S(2)}) copy-start(f32[16,256]{1,0:T(8,128)} %obs_weights.1) | copy-start | bytes 49156
  6.5 0.7 %copy-start.6 = (f32[4,4]{1,0:T(4,128)S(1)}, f32[4,4]{1,0:T(4,128)}, u32[]{:S(2)}) copy-start(f32[4,4]{1,0:T(4,128)} %coupling_s.1) | copy-start | bytes 196
  7.2 0.7 %copy-start.7 = (s32[16]{0:T(128)S(1)}, s32[16]{0:T(128)}, u32[]{:S(2)}) copy-start(s32[16]{0:T(128)} %owner_s.1) | copy-start | bytes 196
  7.9 0.7 %copy-start.8 = (s32[16]{0:T(128)S(1)}, s32[16]{0:T(128)}, u32[]{:S(2)}) copy-start(s32[16]{0:T(128)} %slot_s.1) | copy-start | bytes 196
  8.5 0.7 %copy-start.9 = (s32[16]{0:T(128)S(1)}, s32[16]{0:T(128)}, u32[]{:S(2)}) copy-start(s32[16]{0:T(128)} %counts_s.1) | copy-start | bytes 196
  9.2 0.7 %copy-start.10 = (s32[16]{0:T(128)S(1)}, s32[16]{0:T(128)}, u32[]{:S(2)}) copy-start(s32[16]{0:T(128)} %swath_s.1) | copy-start | bytes 196
  9.8 0.7 %copy-start.11 = (f32[8]{0:T(128)S(1)}, f32[8]{0:T(128)}, u32[]{:S(2)}) copy-start(f32[8]{0:T(128)} %scale_s.1) | copy-start | bytes 100

commit v2 on v1

--- a/solution.py
+++ b/solution.py
@@ -24,6 +24,20 @@
 
 def kernel(
     sizes,
+    owner_hbm,
+    slot_hbm,
+    counts_hbm,
+    swath_hbm,
+    scale_hbm,
+    coupling_hbm,
+    bg_hbm,
+    decay_hbm,
+    edge_hbm,
+    tiles_hbm,
+    values_hbm,
+    weights_hbm,
+    sol_out,
+    res_out,
     owner_s,
     slot_s,
     counts_s,
@@ -33,11 +47,8 @@
     bg,
     decay,
     edge,
-    tiles_hbm,
     obs_values,
     obs_weights,
-    sol_out,
-    res_out,
     tiles,
     ve,
     hn,
@@ -93,8 +104,27 @@
     has_north = (my_row > 0).astype(f32)
     has_south = (my_row < row_n - 1).astype(f32)
 
-    load = pltpu.make_async_copy(tiles_hbm, tiles, load_sem)
-    load.start()
+    loads = [
+        pltpu.make_async_copy(src, dst, load_sem.at[k])
+        for k, (src, dst) in enumerate(
+            (
+                (edge_hbm, edge),
+                (bg_hbm, bg),
+                (owner_hbm, owner_s),
+                (slot_hbm, slot_s),
+                (counts_hbm, counts_s),
+                (swath_hbm, swath_s),
+                (scale_hbm, scale_s),
+                (coupling_hbm, coupling_s),
+                (values_hbm, obs_values),
+                (weights_hbm, obs_weights),
+                (decay_hbm, decay),
+                (tiles_hbm, tiles),
+            )
+        )
+    ]
+    for load in loads:
+        load.start()
 
     barrier = pltpu.get_barrier_semaphore()
 
@@ -229,11 +259,40 @@
     wide_iota = lax.broadcasted_iota(jnp.int32, (pos_n, patch), 0)
     obs_iota = lax.broadcasted_iota(jnp.int32, (pos_n, obs_len), 1)
 
+    loads[0].wait()
+    for e in range(4):
+        put_field(1, e, edge[e])
+    loads[1].wait()
     for f in range(fields):
         put_field(0, f, bg[f])
-    for e in range(4):
-        put_field(1, e, edge[e])
-
+
+    def spread(value, t):
+        return jnp.where(wide_iota == positions[t], value, 0.0).astype(bf16)
+
+    def forward(value):
+        acc = None
+        for t in range(tile_n):
+            term = lax.dot_general(
+                spread(value, t), tiles[t], (((1,), (1,)), ((), ())), preferred_element_type=f32
+            )
+            acc = term if acc is None else acc + term
+        return acc
+
+    def adjoint(value):
+        acc = None
+        for t in range(tile_n):
+            term = lax.dot_general(
+                spread(value, t), tiles[t], (((1,), (0,)), ((), ())), preferred_element_type=f32
+            )
+            acc = term if acc is None else acc + term
+        return acc
+
+    pl.semaphore_wait(barrier, dev_n - 1)
+    halo_start(1)
+    halo_start(0)
+
+    for load in loads[2:11]:
+        load.wait()
     positions = []
     for t in range(tile_n):
         rank = jnp.int32(0)
@@ -258,33 +317,9 @@
     ask[...] = asked.reshape(lon_n, SLOT_ROWS, 128)
     weight[...] = weight_all
 
-    def spread(value, t):
-        return jnp.where(wide_iota == positions[t], value, 0.0).astype(bf16)
-
-    def forward(value):
-        acc = None
-        for t in range(tile_n):
-            term = lax.dot_general(
-                spread(value, t), tiles[t], (((1,), (1,)), ((), ())), preferred_element_type=f32
-            )
-            acc = term if acc is None else acc + term
-        return acc
-
-    def adjoint(value):
-        acc = None
-        for t in range(tile_n):
-            term = lax.dot_general(
-                spread(value, t), tiles[t], (((1,), (0,)), ((), ())), preferred_element_type=f32
-            )
-            acc = term if acc is None else acc + term
-        return acc
-
-    pl.semaphore_wait(barrier, dev_n - 1)
-    halo_start(1)
-    halo_start(0)
     swap_start(0, ask, req)
 
-    load.wait()
+    loads[11].wait()
     scaled = (weight_all * values_all).astype(bf16).astype(f32)
     zs[0] = adjoint(scaled).reshape(lon_n, SLOT_ROWS, patch)
     swap_start(1, zs.at[0], zr.at[0])
@@ -479,16 +514,26 @@
     patch_n = fields * rows * cols // patch
     halos = 4 + 2 * ITERS
     f32, bf16 = jnp.float32, jnp.bfloat16
-    smem = pl.BlockSpec(memory_space=pltpu.SMEM)
     vmem = pl.BlockSpec(memory_space=pltpu.VMEM)
     dma = pltpu.SemaphoreType.DMA
     shape = jax.ShapeDtypeStruct((fields, rows, cols), f32)
     return pl.pallas_call(
         functools.partial(kernel, sizes),
         out_shape=(shape, shape),
-        in_specs=[smem] * 6 + [vmem] * 3 + [pl.BlockSpec(memory_space=pl.ANY)] + [vmem] * 2,
+        in_specs=[pl.BlockSpec(memory_space=pltpu.HBM)] * 12,
         out_specs=(vmem, vmem),
         scratch_shapes=[
+            pltpu.SMEM(tile_owner.shape, jnp.int32),
+            pltpu.SMEM(tile_slot.shape, jnp.int32),
+            pltpu.SMEM(obs_counts.shape, jnp.int32),
+            pltpu.SMEM(swath_ids.shape, jnp.int32),
+            pltpu.SMEM(swath_scale.shape, f32),
+            pltpu.SMEM(coupling.shape, f32),
+            pltpu.VMEM(background.shape, f32),
+            pltpu.VMEM(decay_sq.shape, f32),
+            pltpu.VMEM(edge_weight.shape, f32),
+            pltpu.VMEM(obs_values.shape, f32),
+            pltpu.VMEM(obs_weights.shape, f32),
             pltpu.VMEM((tile_n, obs_len, patch), bf16),
             pltpu.VMEM((halos, fields, rows, ext), f32),
             pltpu.VMEM((halos, fields, ext), f32),
@@ -519,10 +564,10 @@
             dma((2 + 2 * ITERS,)),
             dma((2 * ITERS,)),
             dma((2 * ITERS,)),
-            dma(()),
+            dma((12,)),
         ],
         compiler_params=pltpu.CompilerParams(
-            collective_id=0, has_side_effects=True, vmem_limit_bytes=40 * 1024 * 1024
+            collective_id=0, has_side_effects=True, vmem_limit_bytes=67043328
         ),
     )(
         tile_owner,

time: 65.1 us -> 57.1 us (0.88)
  local copies, waits for them, and re-layouts: 11.2 us -> 3.34 us
    unnamed x26 -> x2, local copies, waits for them, and re-layouts: 11.2 us -> 3.34 us
where the time goes in v2:
time: 57.1 us; the launch traced here: 56.9 us
  Pallas kernels  52.9 us (93%)
  local copies, waits for them, and re-layouts  3.34 us (6%)
  between operations  0.64 us (1%)
    pallas_call x1, Pallas kernels, on_device(): pl.pallas_call(functools.partial(kernel, sizes), out_shape=(shape, shape)...  52.9 us
    unnamed x2, local copies, waits for them, and re-layouts  3.34 us

profile of v2, /device:TPU:0, one launch (start us, length us, event | category | flops | bytes accessed | tf_op | source)
XLA Modules:
  0.0 56.9 jit_solution(5925137872295401751)
XLA Ops:
  0.6 52.9 %shard_map.131 = (f32[4,8,2048]{2,1,0:T(8,128)}, f32[4,8,2048]{2,1,0:T(8,128)}) custom-call(s32[16]{0:T(128)} %owner_hbm.1, s32[16]{0:T(128)} %slot_hbm.1, s32[16]{0:T(128)} %counts_hbm.1, s32[16]{0:T(128)} %swath_hbm.1, f32[8]{0:T(128)} %scale_hbm.1, f32[4,4]{1,0:T(4,128)} %coupling_hbm.1, f32[4,8,2048]{2,1,0:T(8,128)} %bg_hbm.1, f32[4,8,2048]{2,1,0:T(8,128)} %decay_hbm.1, ...), custom_call_target="tpu_custom_call" | custom-call | tf_op jit(solution)/shard_map/pallas_call | solution.py:520
  53.5 1.7 %copy.16 = f32[4,8,2048]{2,1,0:T(8,128)} copy(f32[4,8,2048]{2,1,0:T(8,128)} %get-tuple-element.4) | data formatting | bytes 524288
  55.2 1.7 %copy.17 = f32[4,8,2048]{2,1,0:T(8,128)} copy(f32[4,8,2048]{2,1,0:T(8,128)} %get-tuple-element.5) | data formatting | bytes 524288

commit v3 on v2

--- a/solution.py
+++ b/solution.py
@@ -55,6 +55,8 @@
     hs,
     p0,
     p7,
+    ew_out,
+    ew_in,
     coef,
     diag,
     pe,
@@ -142,8 +144,8 @@
 
     def halo_copies(h):
         pairs = (
-            (ve.at[h, :, :, pl.ds(EDGE, EDGE)], ve.at[h, :, :, right], west, my_row),
-            (ve.at[h, :, :, pl.ds(cols, EDGE)], ve.at[h, :, :, left], east, my_row),
+            (ew_out.at[h, 0], ew_in.at[h, 0], west, my_row),
+            (ew_out.at[h, 1], ew_in.at[h, 1], east, my_row),
             (p0.at[h], hs.at[h, :, center], my_lon, north),
             (p7.at[h], hn.at[h, :, center], my_lon, south),
             (p0.at[h, :, first], hs.at[h, :, right], west, north),
@@ -163,10 +165,22 @@
             for k, (src, dst, lon, row) in enumerate(pairs)
         ]
 
-    def put_field(h, f, value):
-        ve[h, f, :, EDGE : EDGE + cols] = value
-        p0[h, f : f + 1, :] = value[0:1]
-        p7[h, f : f + 1, :] = value[rows - 1 : rows]
+    lane = lax.broadcasted_iota(jnp.int32, (rows, EDGE), 1)
+
+    def turn(value, by):
+        return pltpu.roll(value, by % EDGE, 1) if by % EDGE else value
+
+    def put_fields(h, values):
+        to_west = jnp.zeros((rows, EDGE), f32)
+        to_east = to_west
+        for f, value in enumerate(values):
+            ve[h, f, :, EDGE : EDGE + cols] = value
+            p0[h, f : f + 1, :] = value[0:1]
+            p7[h, f : f + 1, :] = value[rows - 1 : rows]
+            to_west = jnp.where(lane == f, turn(value[:, 0:EDGE], f), to_west)
+            to_east = jnp.where(lane == f, turn(value[:, cols - EDGE : cols], f + 1), to_east)
+        ew_out[h, 0] = to_west
+        ew_out[h, 1] = to_east
 
     def halo_start(h):
         for copy in halo_copies(h):
@@ -175,13 +189,16 @@
     def halo_wait(h):
         for copy in halo_copies(h):
             copy.wait_recv()
+        for f in range(fields):
+            ve[h, f, :, 0:EDGE] = turn(ew_in[h, 1], EDGE - 1 - f)
+            ve[h, f, :, EDGE + cols : ext] = turn(ew_in[h, 0], EDGE - f)
 
     def swap_start(number, out, into):
         def send(k):
             to = (my_lon + k) % lon_n
             pltpu.make_async_remote_copy(
-                src_ref=out.at[to],
-                dst_ref=into.at[my_lon],
+                src_ref=out.at[to, pl.ds(0, CAP)],
+                dst_ref=into.at[my_lon, pl.ds(0, CAP)],
                 send_sem=ex_send.at[number],
                 recv_sem=ex_recv.at[number],
                 device_id=device(to, my_row),
@@ -192,7 +209,7 @@
         into[my_lon] = out[my_lon]
 
     def swap_wait(sems, number, buffer):
-        some = buffer.at[pl.ds(0, lon_n - 1)]
+        some = buffer.at[pl.ds(0, lon_n - 1), pl.ds(0, CAP)]
         pltpu.make_async_copy(some, some, sems.at[number]).wait()
 
     def total_start(number, value):
@@ -259,12 +276,12 @@
     wide_iota = lax.broadcasted_iota(jnp.int32, (pos_n, patch), 0)
     obs_iota = lax.broadcasted_iota(jnp.int32, (pos_n, obs_len), 1)
 
+    in_use = lax.rem(wide_iota, SLOT_ROWS) < CAP
+
     loads[0].wait()
-    for e in range(4):
-        put_field(1, e, edge[e])
+    put_fields(1, [edge[e] for e in range(4)])
     loads[1].wait()
-    for f in range(fields):
-        put_field(0, f, bg[f])
+    put_fields(0, [bg[f] for f in range(fields)])
 
     def spread(value, t):
         return jnp.where(wide_iota == positions[t], value, 0.0).astype(bf16)
@@ -356,12 +373,12 @@
 
     halo_wait(0)
     first_pass = [apply_l(f, ve[0, f], up_of(0, f), down_of(0, f)) for f in range(fields)]
-    for f in range(fields):
-        put_field(2, f, mixed(first_pass, f))
+    put_fields(2, [mixed(first_pass, f) for f in range(fields)])
     halo_start(2)
 
     swap_wait(ex_recv, 0, req)
     wanted = req[...].reshape(pos_n, 128)
+    wanted = jnp.where(lax.rem(row_iota, SLOT_ROWS) < CAP, wanted, -1)
     wanted = jnp.concatenate([wanted] * (patch_n // 128), axis=1)
     picked = wanted == lax.broadcasted_iota(jnp.int32, (pos_n, patch_n), 1)
     chosen = jnp.where(picked, 1.0, 0.0)
@@ -371,7 +388,7 @@
     scatter_oh[...] = chosen.T.astype(bf16)
 
     def placed(number):
-        arrived = zr[number].reshape(pos_n, patch)
+        arrived = jnp.where(in_use, zr[number].reshape(pos_n, patch), 0.0)
         if pos_n < 128:
             arrived = jnp.concatenate([arrived, jnp.zeros((128 - pos_n, patch), f32)], axis=0)
         high, middle, low = split3(arrived)
@@ -395,8 +412,8 @@
         qp[f] = second[f]
     swap_wait(ex_recv, 1, zr.at[0])
     blocks = placed(0)
+    put_fields(3, [qp[f] + placed_field(blocks, f) for f in range(fields)])
     for f in range(fields):
-        put_field(3, f, qp[f] + placed_field(blocks, f))
         sol_out[f] = jnp.zeros((rows, cols), f32)
     pe[...] = jnp.zeros_like(pe)
     pn[...] = jnp.zeros_like(pn)
@@ -405,12 +422,12 @@
 
     def iterate(it, norm_before):
         h_r, h_u = 3 + 2 * it, 4 + 2 * it
-        halo_start(h_r)
         squares = jnp.zeros((1, 128), f32)
         for f in range(fields):
             value = ve[h_r, f, :, EDGE : EDGE + cols]
             squares = squares + lanes_of(value * value)
         total_start(2 * it, squares)
+        halo_start(h_r)
         stacked = jnp.concatenate(
             [
                 ve[h_r, f, :, EDGE + c * patch : EDGE + (c + 1) * patch]
@@ -435,17 +452,17 @@
             pe[f] = ve[h_r, f] + ratio * pe[f]
         pn[...] = hn[h_r] * has_north + ratio * pn[...]
         ps_[...] = hs[h_r] * has_south + ratio * ps_[...]
-        seen = xr[it].reshape(pos_n, patch) + ratio * xp[...]
+        seen = jnp.where(in_use, xr[it].reshape(pos_n, patch), 0.0) + ratio * xp[...]
         xp[...] = seen
 
         first_pass = [
             apply_l(f, pe[f], pn[f : f + 1, :], ps_[f : f + 1, :]) for f in range(fields)
         ]
         curve = jnp.zeros((1, 128), f32)
+        second_in = [mixed(first_pass, f) for f in range(fields)]
+        put_fields(h_u, second_in)
         for f in range(fields):
-            value = mixed(first_pass, f)
-            put_field(h_u, f, value)
-            curve = curve + lanes_of(value * first_pass[f])
+            curve = curve + lanes_of(second_in[f] * first_pass[f])
         halo_start(h_u)
 
         applied = forward(seen)
@@ -461,10 +478,12 @@
         swap_wait(ex_recv, 3 + 2 * it, zr.at[it + 1])
         blocks = placed(it + 1)
         step = norm / total(2 * it + 1)
+        left_over = []
         for f in range(fields):
             sol_out[f] = sol_out[f] + step * pe[f, :, EDGE : EDGE + cols]
             image = qp[f] + placed_field(blocks, f)
-            put_field(h_r + 2, f, ve[h_r, f, :, EDGE : EDGE + cols] - step * image)
+            left_over.append(ve[h_r, f, :, EDGE : EDGE + cols] - step * image)
+        put_fields(h_r + 2, left_over)
         return norm
 
     lax.fori_loop(0, ITERS, iterate, jnp.full((1, 1), 1.0, f32))
@@ -516,7 +535,7 @@
     f32, bf16 = jnp.float32, jnp.bfloat16
     vmem = pl.BlockSpec(memory_space=pltpu.VMEM)
     dma = pltpu.SemaphoreType.DMA
-    shape = jax.ShapeDtypeStruct((fields, rows, cols), f32)
+    shape = pltpu.VMEM((fields, rows, cols), f32)
     return pl.pallas_call(
         functools.partial(kernel, sizes),
         out_shape=(shape, shape),
@@ -540,6 +559,8 @@
             pltpu.VMEM((halos, fields, ext), f32),
             pltpu.VMEM((halos, fields, cols), f32),
             pltpu.VMEM((halos, fields, cols), f32),
+            pltpu.VMEM((halos, 2, rows, EDGE), f32),
+            pltpu.VMEM((halos, 2, rows, EDGE), f32),
             pltpu.VMEM((8, rows, ext), f32),
             pltpu.VMEM((fields, rows, ext), f32),
             pltpu.VMEM((fields, rows, ext), f32),
@@ -567,7 +588,7 @@
             dma((12,)),
         ],
         compiler_params=pltpu.CompilerParams(
-            collective_id=0, has_side_effects=True, vmem_limit_bytes=67043328
+            collective_id=0, has_side_effects=True, vmem_limit_bytes=67043328 - 3 * 2**20
         ),
     )(
         tile_owner,

time: 57.1 us -> 52.3 us (0.916)
  Pallas kernels: 52.9 us -> 50.1 us
  local copies, waits for them, and re-layouts: 3.34 us -> 1.41 us
    pallas_call x1, Pallas kernels: 52.9 us -> 50.1 us  [on_device(): pl.pallas_call(functools.partial(kernel, sizes), out_shape=(shape, shape)...]
    unnamed x2, local copies, waits for them, and re-layouts: 3.34 us -> 1.41 us
where the time goes in v3:
time: 52.3 us; the launch traced here: 52.2 us
  Pallas kernels  50.1 us (96%)
  local copies, waits for them, and re-layouts  1.41 us (3%)
  between operations  0.64 us (1%)
    pallas_call x1, Pallas kernels, on_device(): pl.pallas_call(functools.partial(kernel, sizes), out_shape=(shape, shape)...  50.1 us
    unnamed x2, local copies, waits for them, and re-layouts  1.41 us

profile of v3, /device:TPU:0, one launch (start us, length us, event | category | flops | bytes accessed | tf_op | source)
XLA Modules:
  0.0 52.2 jit_solution(8646081001579739248)
XLA Ops:
  0.6 50.1 %shard_map.131 = (f32[4,8,2048]{2,1,0:T(8,128)S(1)}, f32[4,8,2048]{2,1,0:T(8,128)S(1)}) custom-call(s32[16]{0:T(128)} %owner_hbm.1, s32[16]{0:T(128)} %slot_hbm.1, s32[16]{0:T(128)} %counts_hbm.1, s32[16]{0:T(128)} %swath_hbm.1, f32[8]{0:T(128)} %scale_hbm.1, f32[4,4]{1,0:T(4,128)} %coupling_hbm.1, f32[4,8,2048]{2,1,0:T(8,128)} %bg_hbm.1, ...), custom_call_target="tpu_custom_call" | custom-call | tf_op jit(solution)/shard_map/pallas_call | solution.py:539
  50.8 0.7 %copy.16 = f32[4,8,2048]{2,1,0:T(8,128)} copy(f32[4,8,2048]{2,1,0:T(8,128)S(1)} %get-tuple-element.2) | data formatting | bytes 524288
  51.5 0.7 %copy.17 = f32[4,8,2048]{2,1,0:T(8,128)} copy(f32[4,8,2048]{2,1,0:T(8,128)S(1)} %get-tuple-element.3) | data formatting | bytes 524288

commit v4 on v3

--- a/solution.py
+++ b/solution.py
@@ -15,7 +15,7 @@
 
 
 def loop(low, high, body):
-    if high - low <= 4:
+    if high - low <= 16:
         for k in range(low, high):
             body(k)
     else:

time: 52.3 us -> 50.2 us (0.960)
  Pallas kernels: 50.1 us -> 48 us
    pallas_call x1, Pallas kernels: 50.1 us -> 48 us  [on_device(): pl.pallas_call(functools.partial(kernel, sizes), out_shape=(shape, shape)...]
where the time goes in v4:
time: 50.2 us; the launch traced here: 50.1 us
  Pallas kernels  48 us (96%)
  local copies, waits for them, and re-layouts  1.41 us (3%)
  between operations  0.64 us (1%)
    pallas_call x1, Pallas kernels, on_device(): pl.pallas_call(functools.partial(kernel, sizes), out_shape=(shape, shape)...  48 us
    unnamed x2, local copies, waits for them, and re-layouts  1.41 us

profile of v4, /device:TPU:0, one launch (start us, length us, event | category | flops | bytes accessed | tf_op | source)
XLA Modules:
  0.0 50.1 jit_solution(13376834271338432185)
XLA Ops:
  0.6 48.0 %shard_map.131 = (f32[4,8,2048]{2,1,0:T(8,128)S(1)}, f32[4,8,2048]{2,1,0:T(8,128)S(1)}) custom-call(s32[16]{0:T(128)} %owner_hbm.1, s32[16]{0:T(128)} %slot_hbm.1, s32[16]{0:T(128)} %counts_hbm.1, s32[16]{0:T(128)} %swath_hbm.1, f32[8]{0:T(128)} %scale_hbm.1, f32[4,4]{1,0:T(4,128)} %coupling_hbm.1, f32[4,8,2048]{2,1,0:T(8,128)} %bg_hbm.1, ...), custom_call_target="tpu_custom_call" | custom-call | tf_op jit(solution)/shard_map/pallas_call | solution.py:539
  48.7 0.7 %copy.16 = f32[4,8,2048]{2,1,0:T(8,128)} copy(f32[4,8,2048]{2,1,0:T(8,128)S(1)} %get-tuple-element.2) | data formatting | bytes 524288
  49.4 0.7 %copy.17 = f32[4,8,2048]{2,1,0:T(8,128)} copy(f32[4,8,2048]{2,1,0:T(8,128)S(1)} %get-tuple-element.3) | data formatting | bytes 524288
